TPU v7x, 512 devices: a whole 4x8x8 slice. The times are simulated.
512 devices in a mesh: ctx: 64 (over z, y_hi, core), exp: 8 (over x, y_lo).
Axes of the slice: x: 4, y: 8 (y_hi: 4, y_lo: 2; y = y_hi * 2 + y_lo), z: 8, core: 2. Of those that a mesh axis runs over, the one named last changes fastest.
Arguments:
- residual: bfloat16 [4096, 2048], P('ctx', 'exp'), may hold values from -60 to 60
- queries: bfloat16 [4096, 2048], P('ctx', 'exp'), may hold values from -6.5 to 6.5
- keys: bfloat16 [4096, 2048], P('ctx', 'exp'), may hold values from -6.5 to 6.5
- values: bfloat16 [4096, 2048], P('ctx', 'exp'), may hold values from -6 to 6
- out_proj: bfloat16 [2048, 2048], P(None, 'exp'), may hold values from -0.5 to 0.5
- norm_gain: float32 [2048], replicated, may hold values from 0.1 to 1.9
- w_gate: bfloat16 [8, 2048, 8192], P('exp', None, 'ctx'), may hold values from -0.125 to 0.125
- w_up: bfloat16 [8, 2048, 8192], P('exp', None, 'ctx'), may hold values from -0.125 to 0.125
- w_down: bfloat16 [8, 8192, 2048], P('exp', 'ctx'), may hold values from -0.0625 to 0.0625
- routes: int32 [4096, 1], P('ctx'), may hold values from 0 to 7; in each aligned block of 64 rows (0 to 63, 64 to 127, ...) at most 8 rows name the same one
- block_mask: int32 [32, 32], replicated, may hold values from 0 to 1, as said below
Outputs:
- mixed: bfloat16 [8, 512, 2048], P('exp', 'ctx')
Inputs may be any that keep to these rules, and one draw needn't show every extreme that they name: `routes`: each stored row is named by exactly 8 of the 64 rows of one index of ctx. `block_mask`: every diagonal entry is 1.
All inputs are finite; a program needn't handle non-finite values.
Results may differ from a plain program's by a relative error of at most 0.006.
Values may be sent and summed in bfloat16 or wider, within the bound.
A program may use at most 64 MiB of HBM per device.

v0:
```python
import math

import jax
import jax.numpy as jnp
from jax import lax
from jax.sharding import PartitionSpec as P

HD = 128
BLK = 128


def body(
    residual, queries, keys, values, out_proj, norm_gain, w_gate, w_up, w_down, routes, block_mask
):
    local_tokens = residual.shape[0]
    local_width = queries.shape[1]
    heads_here = local_width // HD
    blocks_all = block_mask.shape[0]
    expert_count = lax.axis_size("exp")
    per_expert = local_tokens // expert_count
    scaling = 1.0 / math.sqrt(HD)
    ctx_place = lax.axis_index("ctx")
    query_pos = ctx_place * local_tokens + jnp.arange(local_tokens, dtype=jnp.int32)
    query_blocks = jax.nn.one_hot(query_pos // BLK, blocks_all, dtype=jnp.float32)
    query_mask = jnp.dot(query_blocks, block_mask.astype(jnp.float32))
    query_three = queries.reshape(local_tokens, heads_here, HD)
    key_piece = lax.all_gather(keys, "ctx", axis=0, tiled=True)
    value_piece = lax.all_gather(values, "ctx", axis=0, tiled=True)
    count_here = key_piece.shape[0]
    key_pos = jnp.arange(count_here, dtype=jnp.int32)
    key_blocks = jax.nn.one_hot(key_pos // BLK, blocks_all, dtype=jnp.float32)
    allowed = jnp.dot(query_mask, key_blocks.T) > 0.5
    top_old = jnp.full((heads_here, local_tokens), -1e30, jnp.float32)
    key_three = key_piece.reshape(count_here, heads_here, HD)
    value_three = value_piece.reshape(count_here, heads_here, HD)
    scores = (
        jnp.einsum("qhd,khd->hqk", query_three, key_three, preferred_element_type=jnp.float32)
        * scaling
    )
    scores = jnp.where(allowed[None], scores, -1e30)
    top_new = jnp.maximum(top_old, jnp.max(scores, axis=2))
    exponent = jnp.where(allowed[None], jnp.exp(scores - top_new[:, :, None]), 0.0)
    total_new = jnp.sum(exponent, axis=2)
    product = jnp.einsum(
        "hqk,khd->hqd",
        exponent.astype(jnp.bfloat16),
        value_three,
        preferred_element_type=jnp.float32,
    )
    attended = (product / total_new[:, :, None]).astype(jnp.bfloat16)
    attended = attended.transpose(1, 0, 2).reshape(local_tokens, local_width)
    projected = jnp.dot(
        lax.all_gather(attended, "exp", axis=1, tiled=True),
        out_proj,
        preferred_element_type=jnp.float32,
    )
    hidden = (residual.astype(jnp.float32) + projected).astype(jnp.bfloat16)
    target = routes[:, 0]
    token_ids = jnp.arange(local_tokens, dtype=jnp.int32)
    earlier = (target[:, None] == target[None, :]) & (token_ids[None, :] < token_ids[:, None])
    ranking = jnp.sum(earlier.astype(jnp.int32), axis=1)
    slot_of = target * per_expert + ranking
    slot_ids = jnp.arange(expert_count * per_expert, dtype=jnp.int32)
    placing = (slot_of[None, :] == slot_ids[:, None]).astype(jnp.bfloat16)
    send_buffer = jnp.dot(placing, hidden, preferred_element_type=jnp.float32).astype(jnp.bfloat16)
    send_buffer = send_buffer.reshape(expert_count, per_expert, hidden.shape[1])
    own_rows = lax.all_to_all(send_buffer, "exp", split_axis=0, concat_axis=2, tiled=True)[0]
    values_f = own_rows.astype(jnp.float32)
    meansq = jnp.mean(values_f * values_f, axis=1, keepdims=True)
    normed_own = (values_f * lax.rsqrt(meansq + 1e-05) * norm_gain).astype(jnp.bfloat16)
    normed_rows = lax.all_gather(normed_own, "ctx", axis=0, tiled=True)
    gate_v = jnp.dot(normed_rows, w_gate[0], preferred_element_type=jnp.float32)
    up_v = jnp.dot(normed_rows, w_up[0], preferred_element_type=jnp.float32)
    activ = (jax.nn.silu(gate_v) * up_v).astype(jnp.bfloat16)
    terms = jnp.dot(activ, w_down[0], preferred_element_type=jnp.float32)
    summed = lax.psum_scatter(terms, "ctx", scatter_dimension=0, tiled=True)
    return (own_rows.astype(jnp.float32) + summed).astype(jnp.bfloat16)[None]


def solution(mesh):
    in_specs = (
        P("ctx", "exp"),
        P("ctx", "exp"),
        P("ctx", "exp"),
        P("ctx", "exp"),
        P(None, "exp"),
        P(),
        P("exp", None, "ctx"),
        P("exp", None, "ctx"),
        P("exp", "ctx", None),
        P("ctx", None),
        P(),
    )
    out_specs = P("exp", "ctx", None)
    return jax.shard_map(body, mesh=mesh, in_specs=in_specs, out_specs=out_specs, check_vma=False)
```

profile of v0, /device:TPU:2, one launch (start us, length us, event | category | flops | bytes accessed | tf_op | source)
XLA Modules:
  0.0 478.8 jit_solution(12788094995489610600)
XLA Ops:
  6.5 0.0 copy-start
  6.5 0.0 all-gather.4.cloned.1.call-start
  6.5 0.7 all-gather.4.cloned.1.call-update
  7.3 0.0 all-gather.6.cloned.1.call-start
  7.3 0.7 all-gather.6.cloned.1.call-update
  8.0 0.0 all-gather.8.cloned.1.call-start
  8.1 0.9 convert_reduce_fusion
  9.0 0.7 multiply_add_fusion
  9.7 1.3 convolution_compare_fusion
  10.9 0.0 copy-start.3
  10.9 89.1 %all-gather.4.cloned.1.call-done = bf16[4096,256]{1,0:T(8,128)(2,1)} async-done(((bf16[64,256]{1,0:T(8,128)(2,1)}), bf16[4096,256]{1,0:T(8,128)(2,1)}) %all-gather.4.cloned.1.call-update) | async-done | bytes 2097168 | tf_op jit(solution)/shard_map/all_gather | solution.py:27
  100.0 4.1 copy.25
  104.1 0.0 copy-done.3
  104.1 2.4 fusion.43
  106.5 0.7 fusion.1
  107.1 76.6 %all-gather.6.cloned.1.call-done = bf16[4096,256]{1,0:T(8,128)(2,1)} async-done(((bf16[64,256]{1,0:T(8,128)(2,1)}), bf16[4096,256]{1,0:T(8,128)(2,1)}) %all-gather.6.cloned.1.call-update) | async-done | bytes 2097168 | tf_op jit(solution)/shard_map/all_gather | solution.py:28
  183.7 4.1 copy.28
  187.8 0.0 copy-start.2
  187.8 0.0 copy-start.4
  187.8 2.5 fusion.8
  190.3 26.8 %all_gather.14 = bf16[64,2048]{1,0:T(8,128)(2,1)S(1)} all-gather(bf16[64,256]{1,0:T(8,128)(2,1)S(1)} %bitcast.56), channel_id=1, replica_groups=mesh['ctx'=64,'exp'=8] {'exp'}, dimensions={1}, use_global_device_ids=true | all-gather | bytes 294912 | tf_op jit(solution)/shard_map/all_gather | solution.py:53
  217.1 0.0 copy-done
  217.1 0.0 copy-done.2
  217.1 0.4 fusion.9
  217.5 11.1 %all_to_all.4 = bf16[8,8,256]{2,1,0:T(8,128)(2,1)S(1)} all-to-all(bf16[8,8,256]{2,1,0:T(8,128)(2,1)S(1)} %fusion.9), channel_id=1, replica_groups=mesh['ctx'=64,'exp'=8] {'exp'}, dimensions={0} | all-to-all | bytes 65536 | tf_op jit(solution)/shard_map/all_to_all | solution.py:67
  228.6 0.1 multiply_reduce_fusion
  228.8 0.0 copy-done.4
  228.8 0.7 multiply_convert_fusion
  229.5 0.0 all-gather.8.cloned.1.call-update
  229.5 0.0 reduce-scatter.2.cloned.1.call-start
  229.6 80.5 %all-gather.8.cloned.1.call-done = bf16[512,2048]{1,0:T(8,128)(2,1)} async-done(((bf16[8,2048]{1,0:T(8,128)(2,1)}), bf16[512,2048]{1,0:T(8,128)(2,1)}) %all-gather.8.cloned.1.call-update) | async-done | bytes 2097168 | tf_op jit(solution)/shard_map/all_gather | solution.py:71
  310.0 0.0 copy-start.1
  310.0 2.5 fusion.19
  312.6 0.0 copy-done.1
  312.6 5.4 %fusion.4 = f32[512,2048]{1,0:T(8,128)} fusion(bf16[512,2048]{1,0:T(8,128)(2,1)S(1)} %copy-done.1, bf16[1,128,2048]{2,1,0:T(8,128)(2,1)} %param.19, bf16[1,2048,128]{2,1,0:T(8,128)(2,1)} %param.18, f32[512,128]{1,0:T(8,128)S(1)} %fusion.19), kind=kOutput, calls=%fused_computation.8 | convolution fusion | flops 537264128 | bytes 7602176 | tf_op jit(solution)/shard_map/dot_general | solution.py:75
  318.0 0.0 reduce-scatter.2.cloned.1.call-update
  318.0 152.8 %reduce-scatter.2.cloned.1.call-done = f32[8,2048]{1,0:T(8,128)} async-done(((f32[512,2048]{1,0:T(8,128)}), f32[8,2048]{1,0:T(8,128)}) %reduce-scatter.2.cloned.1.call-update) | async-done | bytes 65552 | tf_op jit(solution)/shard_map/reduce_scatter | solution.py:76
  470.8 1.5 fusion.29
  (6 shorter events, 0.0 us)
Async XLA Ops:
  6.5 210.6 %copy-start = (bf16[2048,256]{1,0:T(8,128)(2,1)S(1)}, bf16[2048,256]{1,0:T(8,128)(2,1)}, u32[]{:S(2)}) copy-start(bf16[2048,256]{1,0:T(8,128)(2,1)} %param.15) | copy-start | bytes 3145732
  6.5 93.5 %all-gather.4.cloned.1.call-start = ((), (), s32[]{:S(2)}) async-start(), calls=%async_computation.2 | async-start | bytes 2129920 | tf_op jit(solution)/shard_map/all_gather | solution.py:27
  7.3 176.5 %all-gather.6.cloned.1.call-start = ((), (), s32[]{:S(2)}) async-start(), calls=%async_computation.3 | async-start | bytes 2129920 | tf_op jit(solution)/shard_map/all_gather | solution.py:28
  8.0 302.0 %all-gather.8.cloned.1.call-start = ((), (), s32[]{:S(2)}) async-start(), calls=%async_computation.4 | async-start | bytes 2129920 | tf_op jit(solution)/shard_map/all_gather | solution.py:71
  10.9 93.2 %copy-start.3 = (bf16[64,256]{1,0:T(8,128)(2,1)S(1)}, bf16[64,256]{1,0:T(8,128)(2,1)}, u32[]{:S(2)}) copy-start(bf16[64,256]{1,0:T(8,128)(2,1)} %param.12) | copy-start | bytes 98308
  187.8 29.3 %copy-start.2 = (bf16[64,256]{1,0:T(8,128)(2,1)S(1)}, bf16[64,256]{1,0:T(8,128)(2,1)}, u32[]{:S(2)}) copy-start(bf16[64,256]{1,0:T(8,128)(2,1)} %param.11) | copy-start | bytes 98308
  187.8 40.9 %copy-start.4 = (f32[2048]{0:T(1024)S(1)}, f32[2048]{0:T(1024)}, u32[]{:S(2)}) copy-start(f32[2048]{0:T(1024)} %param.16) | copy-start | bytes 24580
  229.5 241.3 %reduce-scatter.2.cloned.1.call-start = ((), (), s32[]{:S(2)}) async-start(), calls=%async_computation.5 | async-start | bytes 4259840 | tf_op jit(solution)/shard_map/reduce_scatter | solution.py:76
  310.0 2.5 copy-start.1
Sparse Core Ops, SparseCore 0:
  10.7 89.2 all-gather.3
  103.3 80.3 all-gather.5
  229.6 80.3 all-gather.7
  318.2 152.6 reduce-scatter.1
where the time goes:
time: 479 us
  waiting for transfers between devices  400 us (84%)
  blocking collectives  37.9 us (8%)
  matrix products  14.5 us (3%)
  between operations  13.2 us (3%)
  local copies, waits for them, and re-layouts  8.24 us (2%)
    reduce_scatter x1, waiting for transfers between devices, body(): summed = lax.psum_scatter(terms, 'ctx', scatter_dimension=0, tiled=True)  153 us
    all_gather x1, waiting for transfers between devices, body(): key_piece = lax.all_gather(keys, 'ctx', axis=0, tiled=True)  89.1 us
    all_gather x1, waiting for transfers between devices, body(): normed_rows = lax.all_gather(normed_own, 'ctx', axis=0, tiled=True)  80.5 us
    all_gather x1, waiting for transfers between devices, body(): value_piece = lax.all_gather(values, 'ctx', axis=0, tiled=True)  76.6 us
    all_gather x1, blocking collectives, body(): lax.all_gather(attended, 'exp', axis=1, tiled=True)  26.8 us
    all_to_all x1, blocking collectives, body(): lax.all_to_all(send_buffer, 'exp', split_axis=0, concat_axis=2, tiled=True)  11.1 us
  transfers between devices with their start and end apart: 4, of which 4 were waited for; matrix products, arithmetic and copies ran while one was open for 2% of the time, Pallas kernels for 0%

commit v1 on v0

v1 whole, which is shorter than its diff:
```python
import functools
import math

import jax
import jax.numpy as jnp
from jax import lax
from jax.experimental import pallas as pl
from jax.experimental.pallas import tpu as pltpu
from jax.sharding import PartitionSpec as P

HD = 128
BLK = 128
ROWS_Y = 4
ANY = pl.BlockSpec(memory_space=pl.ANY)
VM = pl.BlockSpec(memory_space=pltpu.VMEM)
MESH = pl.DeviceIdType.MESH
DMA = pltpu.SemaphoreType.DMA


def place(ny):
    me = lax.axis_index("ctx")
    return lax.div(me, 2 * ny), lax.rem(lax.div(me, 2), ny), lax.rem(me, 2)


def greet(peers):
    barrier = pltpu.get_barrier_semaphore()
    for peer in peers:
        pl.semaphore_signal(barrier, inc=1, device_id=peer, device_id_type=MESH)
    pl.semaphore_wait(barrier, len(peers))


def remote(src, dst, send, recv, peer):
    return pltpu.make_async_remote_copy(
        src_ref=src, dst_ref=dst, send_sem=send, recv_sem=recv, device_id=peer, device_id_type=MESH
    )


def spread(nz, ny, at, peer, block, forward):
    z, y, c = at
    y_send, y_recv, f_send, f_recv, b_send, b_recv = block["sems"]
    ref = block["ref"]
    up, down = lax.rem(z + 1, nz), lax.rem(z + nz - 1, nz)
    pending = []

    def go(copy):
        copy.start()
        pending.append(copy)

    for dy in range(1, ny):
        go(remote(ref(z, y), ref(z, y), y_send.at[dy], y_recv.at[dy], peer(z, lax.rem(y + dy, ny), c)))
    half = nz // 2
    events = [(s + j, j, s, d) for j in range(ny) for s in range(half + 1) for d in (1, -1)]
    for _, j, s, d in sorted(events, key=lambda e: (e[0], e[1], e[2], -e[3])):
        yy = lax.rem(y + ny - j, ny)
        longer = 1 if j % 2 == 0 else -1
        hops = half if d == longer else half - 1
        if s > hops or (s == 0 and d == -1):
            continue
        send, recv = (f_send, f_recv) if d == 1 else (b_send, b_recv)
        zz = lax.rem(z + nz - d * s, nz)
        here = ref(zz, yy)
        if s == 0:
            if j > 0:
                remote(here, here, y_send.at[j], y_recv.at[j], peer(z, yy, c)).wait_recv()
            for d0 in (1, -1):
                hops0 = half if d0 == longer else half - 1
                s0, r0 = (f_send, f_recv) if d0 == 1 else (b_send, b_recv)
                if hops0 > 0:
                    go(remote(here, here, s0.at[j, 0], r0.at[j, 0], peer(up if d0 == 1 else down, y, c)))
        else:
            remote(here, here, send.at[j, s - 1], recv.at[j, s - 1], peer(down if d == 1 else up, y, c)).wait_recv()
            if s < hops:
                go(remote(here, here, send.at[j, s], recv.at[j, s], peer(up if d == 1 else down, y, c)))
        forward(zz, yy, j, s if d == 1 else nz - s)
    return pending


def ctx_peer(ny):
    return lambda z, y, c: {"ctx": (z * ny + y) * 2 + c}


def ring_peers(nz, ny, at, peer):
    z, y, c = at
    out = [peer(z, y, 1 - c)]
    out += [peer(z, lax.rem(y + dy, ny), c) for dy in range(1, ny)]
    out += [peer(lax.rem(z + 1, nz), y, c), peer(lax.rem(z + nz - 1, nz), y, c)]
    return out


def keys_kernel(nz, ny, q_ref, kv_ref, qo_ref, g_ref, own, d_send, d_recv, *sems):
    at = z, y, c = place(ny)
    peer = ctx_peer(ny)
    greet(ring_peers(nz, ny, at, peer))
    other = peer(z, y, 1 - c)
    swap_kv = remote(kv_ref.at[1 - c], g_ref.at[z, y, c], d_send.at[0], d_recv.at[0], other)
    swap_q = remote(q_ref.at[1 - c], qo_ref.at[c], d_send.at[1], d_recv.at[1], other)
    swap_kv.start()
    swap_q.start()
    keep_kv = pltpu.make_async_copy(kv_ref.at[c], g_ref.at[z, y, c], own.at[0])
    keep_q = pltpu.make_async_copy(q_ref.at[c], qo_ref.at[c], own.at[1])
    keep_kv.start()
    keep_q.start()
    keep_kv.wait()
    got = g_ref.at[z, y, 1 - c]
    remote(got, got, d_send.at[0], d_recv.at[0], other).wait_recv()
    block = {"ref": lambda zz, yy: g_ref.at[zz, yy], "sems": sems}
    pending = spread(nz, ny, at, peer, block, lambda *a: None)
    for copy in pending:
        copy.wait_send()
    keep_q.wait()
    got_q = qo_ref.at[1 - c]
    remote(got_q, got_q, d_send.at[1], d_recv.at[1], other).wait_recv()
    swap_kv.wait_send()
    swap_q.wait_send()


def rows_kernel(nz, ny, x_ref, g_ref, own, d_send, d_recv, *sems):
    at = z, y, c = place(ny)
    peer = ctx_peer(ny)
    keep = pltpu.make_async_copy(x_ref, g_ref.at[z, y, c], own)
    keep.start()
    greet(ring_peers(nz, ny, at, peer))
    keep.wait()
    other = peer(z, y, 1 - c)
    passed = []

    def forward(zz, yy, j, s):
        here = g_ref.at[zz, yy, c]
        copy = remote(here, here, d_send.at[j, s], d_recv.at[j, s], other)
        copy.start()
        passed.append((copy, zz, yy, j, s))

    block = {"ref": lambda zz, yy: g_ref.at[zz, yy, c], "sems": sems}
    pending = spread(nz, ny, at, peer, block, forward)
    for copy, zz, yy, j, s in passed:
        got = g_ref.at[zz, yy, 1 - c]
        remote(got, got, d_send.at[j, s], d_recv.at[j, s], other).wait_recv()
    for copy, *_ in passed:
        copy.wait_send()
    for copy in pending:
        copy.wait_send()


def ring_sems(nz, ny):
    return [DMA((ny,))] * 2 + [DMA((ny, nz))] * 4


def gather_keys(q2, kv2, nz, ny):
    return pl.pallas_call(
        functools.partial(keys_kernel, nz, ny),
        out_shape=(
            jax.ShapeDtypeStruct(q2.shape, q2.dtype),
            jax.ShapeDtypeStruct((nz, ny) + kv2.shape, kv2.dtype),
        ),
        in_specs=[VM, VM],
        out_specs=(VM, VM),
        scratch_shapes=[DMA((2,)), DMA((2,)), DMA((2,))] + ring_sems(nz, ny),
        compiler_params=pltpu.CompilerParams(collective_id=0, has_side_effects=True),
    )(q2, kv2)


def gather_rows(x, nz, ny):
    return pl.pallas_call(
        functools.partial(rows_kernel, nz, ny),
        out_shape=jax.ShapeDtypeStruct((nz, ny, 2) + x.shape, x.dtype),
        in_specs=[VM],
        out_specs=VM,
        scratch_shapes=[DMA, DMA((ny, nz)), DMA((ny, nz))] + ring_sems(nz, ny),
        compiler_params=pltpu.CompilerParams(collective_id=1, has_side_effects=True),
    )(x)


def heads_kernel(ny, ne, a_ref, o_ref, own, send, recv):
    z, y, c = place(ny)
    e = lax.axis_index("exp")

    def peer(de, dc):
        return {
            "ctx": (z * ny + y) * 2 + lax.rem(c + dc, 2),
            "exp": lax.rem(e + de, ne),
        }

    others = [(de, dc) for de in range(ne) for dc in range(2) if de or dc]
    keep = pltpu.make_async_copy(a_ref.at[c], o_ref.at[e, c], own)
    keep.start()
    greet([peer(de, dc) for de, dc in others])
    copies = []
    for de, dc in others:
        copy = remote(
            a_ref.at[lax.rem(c + dc, 2)], o_ref.at[e, c], send.at[de, dc], recv.at[de, dc], peer(de, dc)
        )
        copy.start()
        copies.append(copy)
    keep.wait()
    for de, dc in others:
        got = o_ref.at[lax.rem(e + ne - de, ne), lax.rem(c + dc, 2)]
        remote(got, got, send.at[de, dc], recv.at[de, dc], peer(de, dc)).wait_recv()
    for copy in copies:
        copy.wait_send()


def share_heads(a, ny, ne):
    return pl.pallas_call(
        functools.partial(heads_kernel, ny, ne),
        out_shape=jax.ShapeDtypeStruct((ne,) + a.shape, a.dtype),
        in_specs=[VM],
        out_specs=VM,
        scratch_shapes=[DMA, DMA((ne, 2)), DMA((ne, 2))],
        compiler_params=pltpu.CompilerParams(collective_id=2, has_side_effects=True),
    )(a)


def sum_kernel(nz, ny, t_ref, h_ref, o_ref, d_buf, s_buf, r_buf, u_buf, v_buf, d_send, d_recv,
               z_send, z_recv, y_send, y_recv):
    z, y, c = place(ny)
    peer = ctx_peer(ny)
    other = peer(z, y, 1 - c)
    peers = [other]
    peers += [peer(lax.rem(z + dz, nz), y, c) for dz in range(1, nz)]
    peers += [peer(z, lax.rem(y + dy, ny), c) for dy in range(1, ny)]
    greet(peers)
    order = sorted(range(1, nz), key=lambda d: -min(d, nz - d)) + [0]
    halves = []
    for dz in order:
        zz = lax.rem(z + dz, nz)
        copy = remote(t_ref.at[zz, :, 1 - c], d_buf.at[dz], d_send.at[dz], d_recv.at[dz], other)
        copy.start()
        halves.append(copy)
    sent = []
    for dz, half in zip(order, halves):
        zz = lax.rem(z + dz, nz)
        half.wait_recv()
        both = t_ref[zz, :, c].astype(jnp.float32) + d_buf[dz].astype(jnp.float32)
        if dz == 0:
            total = both
        else:
            s_buf[dz] = both.astype(jnp.bfloat16)
            copy = remote(s_buf.at[dz], r_buf.at[dz], z_send.at[dz], z_recv.at[dz], peer(zz, y, c))
            copy.start()
            sent.append(copy)
    for copy, dz in zip(sent, order):
        copy.wait_recv()
        total = total + r_buf[dz].astype(jnp.float32)
    u_buf[...] = total.astype(jnp.bfloat16)
    across = []
    for dy in range(1, ny):
        yy = lax.rem(y + dy, ny)
        copy = remote(u_buf.at[yy], v_buf.at[dy], y_send.at[dy], y_recv.at[dy], peer(z, yy, c))
        copy.start()
        across.append(copy)
    result = u_buf[y].astype(jnp.float32)
    for dy, copy in zip(range(1, ny), across):
        copy.wait_recv()
        result = result + v_buf[dy].astype(jnp.float32)
    o_ref[...] = (h_ref[...].astype(jnp.float32) + result).astype(jnp.bfloat16)
    for copy in halves + sent + across:
        copy.wait_send()


def sum_rows(terms, own, nz, ny):
    rows, width = own.shape
    t = terms.reshape(nz, ny, 2, rows, width)
    big = pltpu.VMEM((nz, ny, rows, width), jnp.bfloat16)
    small = pltpu.VMEM((ny, rows, width), jnp.bfloat16)
    return pl.pallas_call(
        functools.partial(sum_kernel, nz, ny),
        out_shape=jax.ShapeDtypeStruct(own.shape, own.dtype),
        in_specs=[VM, VM],
        out_specs=VM,
        scratch_shapes=[big, big, big, small, small, DMA((nz,)), DMA((nz,)), DMA((nz,)), DMA((nz,)),
                        DMA((ny,)), DMA((ny,))],
        compiler_params=pltpu.CompilerParams(collective_id=3, has_side_effects=True),
    )(t, own)


def body(
    residual, queries, keys, values, out_proj, norm_gain, w_gate, w_up, w_down, routes, block_mask
):
    local_tokens = residual.shape[0]
    blocks_all = block_mask.shape[0]
    expert_count = lax.axis_size("exp")
    ny = ROWS_Y
    nz = lax.axis_size("ctx") // (2 * ny)
    per_expert = local_tokens // expert_count
    scaling = 1.0 / math.sqrt(HD)
    ctx_place = lax.axis_index("ctx")
    q2 = queries.reshape(local_tokens, 2, HD).transpose(1, 0, 2)
    kv2 = jnp.concatenate(
        [
            keys.reshape(local_tokens, 2, HD).transpose(1, 0, 2),
            values.reshape(local_tokens, 2, HD).transpose(1, 0, 2),
        ],
        axis=2,
    )
    q_chip, kv_all = gather_keys(q2, kv2, nz, ny)
    chip_tokens = 2 * local_tokens
    q_chip = q_chip.reshape(chip_tokens, HD)
    kv_all = kv_all.reshape(-1, 2 * HD)
    count = kv_all.shape[0]
    query_pos = (ctx_place // 2) * chip_tokens + jnp.arange(chip_tokens, dtype=jnp.int32)
    query_blocks = jax.nn.one_hot(query_pos // BLK, blocks_all, dtype=jnp.float32)
    query_mask = jnp.dot(query_blocks, block_mask.astype(jnp.float32))
    key_pos = jnp.arange(count, dtype=jnp.int32)
    key_blocks = jax.nn.one_hot(key_pos // BLK, blocks_all, dtype=jnp.float32)
    allowed = jnp.dot(query_mask, key_blocks.T) > 0.5
    scores = (
        jnp.einsum("qd,kd->qk", q_chip, kv_all[:, :HD], preferred_element_type=jnp.float32) * scaling
    )
    scores = jnp.where(allowed, scores, -1e30)
    top = jnp.max(scores, axis=1, keepdims=True)
    exponent = jnp.where(allowed, jnp.exp(scores - top), 0.0)
    total = jnp.sum(exponent, axis=1, keepdims=True)
    product = jnp.dot(
        exponent.astype(jnp.bfloat16), kv_all[:, HD:], preferred_element_type=jnp.float32
    )
    attended = (product / total).astype(jnp.bfloat16).reshape(2, local_tokens, HD)
    heads = share_heads(attended, ny, expert_count)
    heads = heads.reshape(2 * expert_count, local_tokens, HD)
    heads = heads.transpose(1, 0, 2).reshape(local_tokens, 2 * expert_count * HD)
    projected = jnp.dot(heads, out_proj, preferred_element_type=jnp.float32)
    hidden = (residual.astype(jnp.float32) + projected).astype(jnp.bfloat16)
    target = routes[:, 0]
    token_ids = jnp.arange(local_tokens, dtype=jnp.int32)
    earlier = (target[:, None] == target[None, :]) & (token_ids[None, :] < token_ids[:, None])
    ranking = jnp.sum(earlier.astype(jnp.int32), axis=1)
    slot_of = target * per_expert + ranking
    slot_ids = jnp.arange(expert_count * per_expert, dtype=jnp.int32)
    placing = (slot_of[None, :] == slot_ids[:, None]).astype(jnp.bfloat16)
    send_buffer = jnp.dot(placing, hidden, preferred_element_type=jnp.float32).astype(jnp.bfloat16)
    send_buffer = send_buffer.reshape(expert_count, per_expert, hidden.shape[1])
    own_rows = lax.all_to_all(send_buffer, "exp", split_axis=0, concat_axis=2, tiled=True)[0]
    values_f = own_rows.astype(jnp.float32)
    meansq = jnp.mean(values_f * values_f, axis=1, keepdims=True)
    normed_own = (values_f * lax.rsqrt(meansq + 1e-05) * norm_gain).astype(jnp.bfloat16)
    normed_rows = gather_rows(normed_own, nz, ny).reshape(-1, normed_own.shape[1])
    gate_v = jnp.dot(normed_rows, w_gate[0], preferred_element_type=jnp.float32)
    up_v = jnp.dot(normed_rows, w_up[0], preferred_element_type=jnp.float32)
    activ = (jax.nn.silu(gate_v) * up_v).astype(jnp.bfloat16)
    terms = jnp.dot(activ, w_down[0], preferred_element_type=jnp.float32).astype(jnp.bfloat16)
    return sum_rows(terms, own_rows, nz, ny)[None]


def solution(mesh):
    in_specs = (
        P("ctx", "exp"),
        P("ctx", "exp"),
        P("ctx", "exp"),
        P("ctx", "exp"),
        P(None, "exp"),
        P(),
        P("exp", None, "ctx"),
        P("exp", None, "ctx"),
        P("exp", "ctx", None),
        P("ctx", None),
        P(),
    )
    out_specs = P("exp", "ctx", None)
    return jax.shard_map(body, mesh=mesh, in_specs=in_specs, out_specs=out_specs, check_vma=False)
```

time: 479 us -> 164 us (0.34)
  the two profiles are of different devices: /device:TPU:2 before, /device:TPU:8 now
where the time goes in v1:
time: 164 us; the launch traced here: 163 us
  Pallas kernels  133 us (81%)
  matrix products  12.3 us (8%)
  blocking collectives  9.82 us (6%)
  local copies, waits for them, and re-layouts  5.72 us (3%)
  other arithmetic  2.31 us (1%)
    pallas_call x1, Pallas kernels, gather_keys(): pl.pallas_call(functools.partial(keys_kernel, nz, ny), out_shape=(jax.Sha...  47.8 us
    pallas_call x1, Pallas kernels, sum_rows(): pl.pallas_call(functools.partial(sum_kernel, nz, ny), out_shape=jax.Shape...  40.6 us
    pallas_call x1, Pallas kernels, gather_rows(): pl.pallas_call(functools.partial(rows_kernel, nz, ny), out_shape=jax.Shap...  33.9 us
    pallas_call x1, Pallas kernels, share_heads(): pl.pallas_call(functools.partial(heads_kernel, ny, ne), out_shape=jax.Sha...  11 us
    all_to_all x1, blocking collectives, body(): lax.all_to_all(send_buffer, 'exp', split_axis=0, concat_axis=2, tiled=True)  9.82 us
    dot_general x1, matrix products, body(): jnp.dot(activ, w_down[0], preferred_element_type=jnp.float32)  4.86 us

profile of v1, /device:TPU:8, one launch (start us, length us, event | category | flops | bytes accessed | tf_op | source)
XLA Modules:
  0.0 163.5 jit_solution(4580896513197424369)
XLA Ops:
  0.0 0.0 copy-start
  0.0 1.5 bitcast_bitcast_fusion.2.q_ref
  1.5 0.8 bitcast_bitcast_fusion
  2.3 0.6 pad_maximum_fusion.kv_ref
  2.9 47.8 %shard_map.109 = (bf16[2,64,128]{2,1,0:T(8,128)(2,1)}, bf16[8,4,2,64,256]{4,3,2,1,0:T(8,128)(2,1)}) custom-call(bf16[2,64,128]{2,1,0:T(8,128)(2,1)} %bitcast_bitcast_fusion.2.q_ref, bf16[2,64,256]{2,1,0:T(8,128)(2,1)} %pad_maximum_fusion.kv_ref), custom_call_target="tpu_custom_call" | custom-call | tf_op jit(solution)/shard_map/pallas_call | solution.py:149
  50.7 0.0 copy-start.4
  50.7 1.4 convolution_compare_fusion
  52.1 0.0 copy-done.4
  52.1 1.8 %fusion.42 = (f32[128]{0:T(128)S(1)}, f32[128,4096]{1,0:T(8,128)S(1)}) fusion(pred[128,4096]{1,0:T(32,128)(4,1)S(1)} %convolution_compare_fusion, bf16[128,128]{1,0:T(8,128)(2,1)S(1)} %bitcast.68, bf16[4096,256]{1,0:T(8,128)(2,1)} %bitcast.65), kind=kOutput, calls=%fused_computation.64 | convolution fusion | flops 135790464 | bytes 3703296 | tf_op jit(solution)/shard_map/qd,kd->qk/dot_general | solution.py:307
  54.0 0.0 copy-start.3
  54.0 0.6 fusion.1
  54.6 0.9 copy-done.3
  55.6 0.0 copy-start.7
  55.6 0.0 copy-start.5
  55.6 1.3 fusion.5
  56.8 0.0 copy-start.6
  56.8 11.0 %shard_map.110 = bf16[8,2,64,128]{3,2,1,0:T(8,128)(2,1)} custom-call(bf16[2,64,128]{2,1,0:T(8,128)(2,1)} %bitcast.69), custom_call_target="tpu_custom_call" | custom-call | tf_op jit(solution)/shard_map/pallas_call | solution.py:203
  67.8 1.1 copy.19
  69.0 0.0 copy-done.7
  69.0 0.2 convert_reduce_fusion
  69.2 0.0 copy-done
  69.2 0.0 copy-done.5
  69.2 0.4 fusion.6
  69.6 9.8 %all_to_all.15 = bf16[8,8,256]{2,1,0:T(8,128)(2,1)S(1)} all-to-all(bf16[8,8,256]{2,1,0:T(8,128)(2,1)S(1)} %fusion.6), channel_id=1, replica_groups=mesh['ctx'=64,'exp'=8] {'exp'}, dimensions={0} | all-to-all | bytes 65536 | tf_op jit(solution)/shard_map/all_to_all | solution.py:331
  79.4 0.0 copy-start.2
  79.4 0.1 multiply_reduce_fusion
  79.5 0.0 copy-done.6
  79.5 0.7 multiply_convert_fusion.x_ref
  80.2 33.9 %shard_map.111 = bf16[8,4,2,8,2048]{4,3,2,1,0:T(8,128)(2,1)} custom-call(bf16[8,2048]{1,0:T(8,128)(2,1)} %multiply_convert_fusion.x_ref), custom_call_target="tpu_custom_call" | custom-call | tf_op jit(solution)/shard_map/pallas_call | solution.py:163
  114.1 0.0 copy-start.1
  114.1 2.5 %fusion.17 = f32[512,128]{1,0:T(8,128)S(1)} fusion(bf16[512,2048]{1,0:T(8,128)(2,1)} %bitcast.58, bf16[1,2048,128]{2,1,0:T(8,128)(2,1)} %param.17), kind=kOutput, calls=%fused_computation.22 | convolution fusion | flops 268435456 | bytes 2883584 | tf_op jit(solution)/shard_map/dot_general | solution.py:336
  116.6 0.0 copy-done.2
  116.7 0.0 copy-done.1
  116.7 4.9 %convolution_convert_fusion = bf16[512,2048]{1,0:T(8,128)(2,1)} fusion(bf16[512,2048]{1,0:T(8,128)(2,1)S(1)} %bitcast.59, bf16[1,128,2048]{2,1,0:T(8,128)(2,1)} %param.19, bf16[1,2048,128]{2,1,0:T(8,128)(2,1)} %param.18, f32[512,128]{1,0:T(8,128)S(1)} %fusion.17), kind=kOutput, calls=%fused_computation.3 | convolution fusion | flops 538312704 | bytes 5505024 | tf_op jit(solution)/shard_map/dot_general | solution.py:339
  121.5 40.6 %shard_map.112 = bf16[8,2048]{1,0:T(8,128)(2,1)} custom-call(bf16[8,4,2,8,2048]{4,3,2,1,0:T(8,128)(2,1)} %bitcast.60, bf16[8,2048]{1,0:T(8,128)(2,1)} %bitcast.64), custom_call_target="tpu_custom_call" | custom-call | tf_op jit(solution)/shard_map/pallas_call | solution.py:265
  162.1 1.4 copy.37
  (4 shorter events, 0.0 us)
Async XLA Ops:
  0.0 69.2 %copy-start = (bf16[2048,256]{1,0:T(8,128)(2,1)S(1)}, bf16[2048,256]{1,0:T(8,128)(2,1)}, u32[]{:S(2)}) copy-start(bf16[2048,256]{1,0:T(8,128)(2,1)} %param.15) | copy-start | bytes 3145732
  50.7 1.5 copy-start.4
  54.0 1.6 copy-start.3
  55.6 13.4 %copy-start.7 = (s32[64,1]{0,1:T(1,128)S(1)}, s32[64,1]{0,1:T(1,128)}, u32[]{:S(2)}) copy-start(s32[64,1]{0,1:T(1,128)} %param.20) | copy-start | bytes 772
  55.6 13.6 %copy-start.5 = (bf16[64,256]{1,0:T(8,128)(2,1)S(1)}, bf16[64,256]{1,0:T(8,128)(2,1)}, u32[]{:S(2)}) copy-start(bf16[64,256]{1,0:T(8,128)(2,1)} %param.11) | copy-start | bytes 98308
  56.8 22.7 %copy-start.6 = (f32[2048]{0:T(1024)S(1)}, f32[2048]{0:T(1024)}, u32[]{:S(2)}) copy-start(f32[2048]{0:T(1024)} %param.16) | copy-start | bytes 24580
  79.4 37.3 %copy-start.2 = (bf16[8,8,256]{2,1,0:T(8,128)(2,1)}, bf16[8,8,256]{2,1,0:T(8,128)(2,1)S(1)}, u32[]{:S(2)}) copy-start(bf16[8,8,256]{2,1,0:T(8,128)(2,1)S(1)} %all_to_all.15) | copy-start | bytes 98308
  114.1 2.6 %copy-start.1 = (bf16[8,4,2,8,2048]{4,3,2,1,0:T(8,128)(2,1)S(1)}, bf16[8,4,2,8,2048]{4,3,2,1,0:T(8,128)(2,1)}, u32[]{:S(2)}) copy-start(bf16[8,4,2,8,2048]{4,3,2,1,0:T(8,128)(2,1)} %shard_map.111) | copy-start | bytes 6291460

commit v2 on v1

--- a/solution.py
+++ b/solution.py
@@ -35,10 +35,9 @@
     )
 
 
-def spread(nz, ny, at, peer, block, forward):
+def spread(nz, ny, at, peer, ref, sems):
     z, y, c = at
-    y_send, y_recv, f_send, f_recv, b_send, b_recv = block["sems"]
-    ref = block["ref"]
+    y_send, y_recv, f_send, f_recv, b_send, b_recv = sems
     up, down = lax.rem(z + 1, nz), lax.rem(z + nz - 1, nz)
     pending = []
 
@@ -71,7 +70,6 @@
             remote(here, here, send.at[j, s - 1], recv.at[j, s - 1], peer(down if d == 1 else up, y, c)).wait_recv()
             if s < hops:
                 go(remote(here, here, send.at[j, s], recv.at[j, s], peer(up if d == 1 else down, y, c)))
-        forward(zz, yy, j, s if d == 1 else nz - s)
     return pending
 
 
@@ -81,17 +79,18 @@
 
 def ring_peers(nz, ny, at, peer):
     z, y, c = at
-    out = [peer(z, y, 1 - c)]
-    out += [peer(z, lax.rem(y + dy, ny), c) for dy in range(1, ny)]
+    out = [peer(z, lax.rem(y + dy, ny), c) for dy in range(1, ny)]
     out += [peer(lax.rem(z + 1, nz), y, c), peer(lax.rem(z + nz - 1, nz), y, c)]
     return out
 
 
-def keys_kernel(nz, ny, q_ref, kv_ref, qo_ref, g_ref, own, d_send, d_recv, *sems):
+def keys_kernel(
+    nz, ny, q_ref, kv_ref, w0, w1, w2, qo_ref, g_ref, p0, p1, p2, own, d_send, d_recv, *sems
+):
     at = z, y, c = place(ny)
     peer = ctx_peer(ny)
-    greet(ring_peers(nz, ny, at, peer))
     other = peer(z, y, 1 - c)
+    greet(ring_peers(nz, ny, at, peer) + [other])
     swap_kv = remote(kv_ref.at[1 - c], g_ref.at[z, y, c], d_send.at[0], d_recv.at[0], other)
     swap_q = remote(q_ref.at[1 - c], qo_ref.at[c], d_send.at[1], d_recv.at[1], other)
     swap_kv.start()
@@ -103,10 +102,17 @@
     keep_kv.wait()
     got = g_ref.at[z, y, 1 - c]
     remote(got, got, d_send.at[0], d_recv.at[0], other).wait_recv()
-    block = {"ref": lambda zz, yy: g_ref.at[zz, yy], "sems": sems}
-    pending = spread(nz, ny, at, peer, block, lambda *a: None)
+    weights = [
+        remote(src, dst, d_send.at[2 + i], d_recv.at[2 + i], other)
+        for i, (src, dst) in enumerate([(w0, p0), (w1, p1), (w2, p2)])
+    ]
+    for copy in weights:
+        copy.start()
+    pending = spread(nz, ny, at, peer, lambda zz, yy: g_ref.at[zz, yy], sems)
     for copy in pending:
         copy.wait_send()
+    for copy in weights:
+        copy.wait()
     keep_q.wait()
     got_q = qo_ref.at[1 - c]
     remote(got_q, got_q, d_send.at[1], d_recv.at[1], other).wait_recv()
@@ -114,30 +120,14 @@
     swap_q.wait_send()
 
 
-def rows_kernel(nz, ny, x_ref, g_ref, own, d_send, d_recv, *sems):
+def rows_kernel(nz, ny, x_ref, g_ref, own, *sems):
     at = z, y, c = place(ny)
     peer = ctx_peer(ny)
-    keep = pltpu.make_async_copy(x_ref, g_ref.at[z, y, c], own)
+    keep = pltpu.make_async_copy(x_ref, g_ref.at[z, y], own)
     keep.start()
     greet(ring_peers(nz, ny, at, peer))
     keep.wait()
-    other = peer(z, y, 1 - c)
-    passed = []
-
-    def forward(zz, yy, j, s):
-        here = g_ref.at[zz, yy, c]
-        copy = remote(here, here, d_send.at[j, s], d_recv.at[j, s], other)
-        copy.start()
-        passed.append((copy, zz, yy, j, s))
-
-    block = {"ref": lambda zz, yy: g_ref.at[zz, yy, c], "sems": sems}
-    pending = spread(nz, ny, at, peer, block, forward)
-    for copy, zz, yy, j, s in passed:
-        got = g_ref.at[zz, yy, 1 - c]
-        remote(got, got, d_send.at[j, s], d_recv.at[j, s], other).wait_recv()
-    for copy, *_ in passed:
-        copy.wait_send()
-    for copy in pending:
+    for copy in spread(nz, ny, at, peer, lambda zz, yy: g_ref.at[zz, yy], sems):
         copy.wait_send()
 
 
@@ -145,27 +135,28 @@
     return [DMA((ny,))] * 2 + [DMA((ny, nz))] * 4
 
 
-def gather_keys(q2, kv2, nz, ny):
+def gather_keys(q2, kv2, weights, nz, ny):
     return pl.pallas_call(
         functools.partial(keys_kernel, nz, ny),
         out_shape=(
             jax.ShapeDtypeStruct(q2.shape, q2.dtype),
             jax.ShapeDtypeStruct((nz, ny) + kv2.shape, kv2.dtype),
+            *(jax.ShapeDtypeStruct(w.shape, w.dtype) for w in weights),
         ),
-        in_specs=[VM, VM],
-        out_specs=(VM, VM),
-        scratch_shapes=[DMA((2,)), DMA((2,)), DMA((2,))] + ring_sems(nz, ny),
+        in_specs=[VM, VM, ANY, ANY, ANY],
+        out_specs=(VM, VM, ANY, ANY, ANY),
+        scratch_shapes=[DMA((2,)), DMA((5,)), DMA((5,))] + ring_sems(nz, ny),
         compiler_params=pltpu.CompilerParams(collective_id=0, has_side_effects=True),
-    )(q2, kv2)
+    )(q2, kv2, *weights)
 
 
 def gather_rows(x, nz, ny):
     return pl.pallas_call(
         functools.partial(rows_kernel, nz, ny),
-        out_shape=jax.ShapeDtypeStruct((nz, ny, 2) + x.shape, x.dtype),
+        out_shape=jax.ShapeDtypeStruct((nz, ny) + x.shape, x.dtype),
         in_specs=[VM],
         out_specs=VM,
-        scratch_shapes=[DMA, DMA((ny, nz)), DMA((ny, nz))] + ring_sems(nz, ny),
+        scratch_shapes=[DMA] + ring_sems(nz, ny),
         compiler_params=pltpu.CompilerParams(collective_id=1, has_side_effects=True),
     )(x)
 
@@ -210,65 +201,107 @@
     )(a)
 
 
-def sum_kernel(nz, ny, t_ref, h_ref, o_ref, d_buf, s_buf, r_buf, u_buf, v_buf, d_send, d_recv,
-               z_send, z_recv, y_send, y_recv):
+def pieces_kernel(ne, x_ref, o_ref, own, send, recv):
+    e = lax.axis_index("exp")
+    keep = pltpu.make_async_copy(x_ref.at[e], o_ref.at[e], own)
+    keep.start()
+    greet([{"exp": lax.rem(e + de, ne)} for de in range(1, ne)])
+    copies = []
+    for de in range(1, ne):
+        to = lax.rem(e + de, ne)
+        copy = remote(x_ref.at[to], o_ref.at[e], send.at[de], recv.at[de], {"exp": to})
+        copy.start()
+        copies.append(copy)
+    keep.wait()
+    for de in range(1, ne):
+        back = lax.rem(e + ne - de, ne)
+        got = o_ref.at[back]
+        remote(got, got, send.at[de], recv.at[de], {"exp": back}).wait_recv()
+    for copy in copies:
+        copy.wait_send()
+
+
+def share_pieces(x, ne):
+    return pl.pallas_call(
+        functools.partial(pieces_kernel, ne),
+        out_shape=jax.ShapeDtypeStruct(x.shape, x.dtype),
+        in_specs=[VM],
+        out_specs=VM,
+        scratch_shapes=[DMA, DMA((ne,)), DMA((ne,))],
+        compiler_params=pltpu.CompilerParams(collective_id=4, has_side_effects=True),
+    )(x)
+
+
+def sum_kernel(nz, ny, t_ref, h_ref, o_ref, rz, ry, uz, uy, vz, vy, *sems):
     z, y, c = place(ny)
+    rz_send, rz_recv, ry_send, ry_recv, vz_send, vz_recv, vy_send, vy_recv = sems
+    half = t_ref.shape[-1] // 2
+    left, right = pl.ds(0, half), pl.ds(half, half)
     peer = ctx_peer(ny)
-    other = peer(z, y, 1 - c)
-    peers = [other]
-    peers += [peer(lax.rem(z + dz, nz), y, c) for dz in range(1, nz)]
-    peers += [peer(z, lax.rem(y + dy, ny), c) for dy in range(1, ny)]
-    greet(peers)
-    order = sorted(range(1, nz), key=lambda d: -min(d, nz - d)) + [0]
-    halves = []
-    for dz in order:
-        zz = lax.rem(z + dz, nz)
-        copy = remote(t_ref.at[zz, :, 1 - c], d_buf.at[dz], d_send.at[dz], d_recv.at[dz], other)
-        copy.start()
-        halves.append(copy)
-    sent = []
-    for dz, half in zip(order, halves):
-        zz = lax.rem(z + dz, nz)
-        half.wait_recv()
-        both = t_ref[zz, :, c].astype(jnp.float32) + d_buf[dz].astype(jnp.float32)
-        if dz == 0:
-            total = both
-        else:
-            s_buf[dz] = both.astype(jnp.bfloat16)
-            copy = remote(s_buf.at[dz], r_buf.at[dz], z_send.at[dz], z_recv.at[dz], peer(zz, y, c))
-            copy.start()
-            sent.append(copy)
-    for copy, dz in zip(sent, order):
+    far_z = sorted(range(1, nz), key=lambda d: -min(d, nz - d))
+    far_y = sorted(range(1, ny), key=lambda d: -min(d, ny - d))
+    to_z = {d: lax.rem(z + d, nz) for d in far_z}
+    to_y = {d: lax.rem(y + d, ny) for d in far_y}
+    greet([peer(to_z[d], y, c) for d in far_z] + [peer(z, to_y[d], c) for d in far_y])
+
+    def send(src, dst, sends, recvs, who):
+        copy = remote(src, dst, sends, recvs, who)
+        copy.start()
+        return copy
+
+    by_z = [
+        send(t_ref.at[to_z[d], :, :, left], rz.at[d], rz_send.at[d], rz_recv.at[d], peer(to_z[d], y, c))
+        for d in far_z
+    ]
+    by_y = [
+        send(t_ref.at[:, to_y[d], :, right], ry.at[d], ry_send.at[d], ry_recv.at[d], peer(z, to_y[d], c))
+        for d in far_y
+    ]
+    total = t_ref[z, :, :, :half].astype(jnp.float32)
+    for d, copy in zip(far_z, by_z):
         copy.wait_recv()
-        total = total + r_buf[dz].astype(jnp.float32)
-    u_buf[...] = total.astype(jnp.bfloat16)
-    across = []
-    for dy in range(1, ny):
-        yy = lax.rem(y + dy, ny)
-        copy = remote(u_buf.at[yy], v_buf.at[dy], y_send.at[dy], y_recv.at[dy], peer(z, yy, c))
-        copy.start()
-        across.append(copy)
-    result = u_buf[y].astype(jnp.float32)
-    for dy, copy in zip(range(1, ny), across):
+        total = total + rz[d].astype(jnp.float32)
+    uz[...] = total.astype(jnp.bfloat16)
+    then_y = [
+        send(uz.at[to_y[d]], vz.at[d], vz_send.at[d], vz_recv.at[d], peer(z, to_y[d], c)) for d in far_y
+    ]
+    total = t_ref[:, y, :, half:].astype(jnp.float32)
+    for d, copy in zip(far_y, by_y):
         copy.wait_recv()
-        result = result + v_buf[dy].astype(jnp.float32)
-    o_ref[...] = (h_ref[...].astype(jnp.float32) + result).astype(jnp.bfloat16)
-    for copy in halves + sent + across:
+        total = total + ry[d].astype(jnp.float32)
+    uy[...] = total.astype(jnp.bfloat16)
+    then_z = [
+        send(uy.at[to_z[d]], vy.at[d], vy_send.at[d], vy_recv.at[d], peer(to_z[d], y, c)) for d in far_z
+    ]
+    result = h_ref[:, :half].astype(jnp.float32) + uz[y].astype(jnp.float32)
+    for d, copy in zip(far_y, then_y):
+        copy.wait_recv()
+        result = result + vz[d].astype(jnp.float32)
+    o_ref[:, :half] = result.astype(jnp.bfloat16)
+    result = h_ref[:, half:].astype(jnp.float32) + uy[z].astype(jnp.float32)
+    for d, copy in zip(far_z, then_z):
+        copy.wait_recv()
+        result = result + vy[d].astype(jnp.float32)
+    o_ref[:, half:] = result.astype(jnp.bfloat16)
+    for copy in by_z + by_y + then_y + then_z:
         copy.wait_send()
 
 
 def sum_rows(terms, own, nz, ny):
     rows, width = own.shape
-    t = terms.reshape(nz, ny, 2, rows, width)
-    big = pltpu.VMEM((nz, ny, rows, width), jnp.bfloat16)
-    small = pltpu.VMEM((ny, rows, width), jnp.bfloat16)
+    half = width // 2
+    t = terms.reshape(nz, ny, rows, width)
+
+    def buf(*lead):
+        return pltpu.VMEM(lead + (rows, half), jnp.bfloat16)
+
     return pl.pallas_call(
         functools.partial(sum_kernel, nz, ny),
         out_shape=jax.ShapeDtypeStruct(own.shape, own.dtype),
         in_specs=[VM, VM],
         out_specs=VM,
-        scratch_shapes=[big, big, big, small, small, DMA((nz,)), DMA((nz,)), DMA((nz,)), DMA((nz,)),
-                        DMA((ny,)), DMA((ny,))],
+        scratch_shapes=[buf(nz, ny), buf(ny, nz), buf(ny), buf(nz), buf(ny), buf(nz)]
+        + [DMA((n,)) for n in (nz, nz, ny, ny, ny, ny, nz, nz)],
         compiler_params=pltpu.CompilerParams(collective_id=3, has_side_effects=True),
     )(t, own)
 
@@ -292,7 +325,8 @@
         ],
         axis=2,
     )
-    q_chip, kv_all = gather_keys(q2, kv2, nz, ny)
+    mine = (w_gate[0], w_up[0], w_down[0])
+    q_chip, kv_all, *partner = gather_keys(q2, kv2, mine, nz, ny)
     chip_tokens = 2 * local_tokens
     q_chip = q_chip.reshape(chip_tokens, HD)
     kv_all = kv_all.reshape(-1, 2 * HD)
@@ -328,15 +362,18 @@
     placing = (slot_of[None, :] == slot_ids[:, None]).astype(jnp.bfloat16)
     send_buffer = jnp.dot(placing, hidden, preferred_element_type=jnp.float32).astype(jnp.bfloat16)
     send_buffer = send_buffer.reshape(expert_count, per_expert, hidden.shape[1])
-    own_rows = lax.all_to_all(send_buffer, "exp", split_axis=0, concat_axis=2, tiled=True)[0]
+    own_rows = share_pieces(send_buffer, expert_count).transpose(1, 0, 2).reshape(per_expert, -1)
     values_f = own_rows.astype(jnp.float32)
     meansq = jnp.mean(values_f * values_f, axis=1, keepdims=True)
     normed_own = (values_f * lax.rsqrt(meansq + 1e-05) * norm_gain).astype(jnp.bfloat16)
     normed_rows = gather_rows(normed_own, nz, ny).reshape(-1, normed_own.shape[1])
-    gate_v = jnp.dot(normed_rows, w_gate[0], preferred_element_type=jnp.float32)
-    up_v = jnp.dot(normed_rows, w_up[0], preferred_element_type=jnp.float32)
-    activ = (jax.nn.silu(gate_v) * up_v).astype(jnp.bfloat16)
-    terms = jnp.dot(activ, w_down[0], preferred_element_type=jnp.float32).astype(jnp.bfloat16)
+    terms = 0.0
+    for gate, up, down in (mine, partner):
+        gate_v = jnp.dot(normed_rows, gate, preferred_element_type=jnp.float32)
+        up_v = jnp.dot(normed_rows, up, preferred_element_type=jnp.float32)
+        activ = (jax.nn.silu(gate_v) * up_v).astype(jnp.bfloat16)
+        terms = terms + jnp.dot(activ, down, preferred_element_type=jnp.float32)
+    terms = terms.astype(jnp.bfloat16)
     return sum_rows(terms, own_rows, nz, ny)[None]
 
 

time: 164 us -> 147 us (0.90)
  Pallas kernels: 133 us -> 123 us
  blocking collectives: 9.82 us -> 0 us
  matrix products: 12.3 us -> 15.1 us
    pallas_call x1, Pallas kernels: 40.6 us -> 23.4 us  [sum_rows(): pl.pallas_call(functools.partial(sum_kernel, nz, ny), out_shape=jax.Shape...]
    all_to_all x1 -> x0, blocking collectives: 9.82 us -> none  [body(): lax.all_to_all(send_buffer, 'exp', split_axis=0, concat_axis=2, tiled=True)]
    pallas_call x0 -> x1, Pallas kernels: none -> 8.66 us  [share_pieces(): pl.pallas_call(functools.partial(pieces_kernel, ne), out_shape=jax.ShapeD...]
    dot_general x2 -> x4, matrix products: 7.39 us -> 9.46 us  [the longest x2 5.82 us: body(): terms = terms + jnp.dot(activ, down, preferred_element_type=jnp.float32)]
    pallas_call x1, Pallas kernels: 33.9 us -> 32.1 us  [gather_rows(): pl.pallas_call(functools.partial(rows_kernel, nz, ny), out_shape=jax.Shap...]
where the time goes in v2:
time: 147 us; the launch traced here: 146 us
  Pallas kernels  123 us (84%)
  matrix products  15.1 us (10%)
  local copies, waits for them, and re-layouts  4.11 us (3%)
  other arithmetic  3.83 us (3%)
    pallas_call x1, Pallas kernels, gather_keys(): pl.pallas_call(functools.partial(keys_kernel, nz, ny), out_shape=(jax.Sha...  47.8 us
    pallas_call x1, Pallas kernels, gather_rows(): pl.pallas_call(functools.partial(rows_kernel, nz, ny), out_shape=jax.Shap...  32.1 us
    pallas_call x1, Pallas kernels, sum_rows(): pl.pallas_call(functools.partial(sum_kernel, nz, ny), out_shape=jax.Shape...  23.4 us
    pallas_call x1, Pallas kernels, share_heads(): pl.pallas_call(functools.partial(heads_kernel, ny, ne), out_shape=jax.Sha...  11 us
    pallas_call x1, Pallas kernels, share_pieces(): pl.pallas_call(functools.partial(pieces_kernel, ne), out_shape=jax.ShapeD...  8.66 us
    dot_general x2, matrix products, body(): terms = terms + jnp.dot(activ, down, preferred_element_type=jnp.float32)  5.82 us
    dot_general x2, matrix products, body(): gate_v = jnp.dot(normed_rows, gate, preferred_element_type=jnp.float32)  3.64 us

profile of v2, /device:TPU:8, one launch (start us, length us, event | category | flops | bytes accessed | tf_op | source)
XLA Modules:
  0.0 146.2 jit_solution(16978990081771146738)
XLA Ops:
  0.0 0.0 copy-start
  0.0 0.0 copy-start.7
  0.0 0.0 copy-start.8
  0.0 0.0 copy-start.6
  0.1 1.5 %convolution_compare_fusion = pred[128,4096]{1,0:T(32,128)(4,1)S(1)} fusion(s32[4096]{0:T(1024)S(1)} %add_select_fusion, s32[128]{0:T(128)S(1)} %and_select_fusion, s32[32,32]{1,0:T(8,128)} %param.21), kind=kOutput, calls=%fused_computation.2 | convolution fusion | flops 34477056 | bytes 545280 | tf_op jit(solution)/shard_map/dot_general | solution.py:339
  1.6 0.0 copy-done.7
  1.6 0.0 copy-done.8
  1.6 0.6 pad_maximum_fusion.kv_ref
  2.3 0.0 copy-done.6
  2.3 0.6 bitcast_bitcast_fusion.2.q_ref
  2.9 47.8 %shard_map.109 = (bf16[2,64,128]{2,1,0:T(8,128)(2,1)}, bf16[8,4,2,64,256]{4,3,2,1,0:T(8,128)(2,1)}, bf16[2048,128]{1,0:T(8,128)(2,1)}, bf16[2048,128]{1,0:T(8,128)(2,1)}, bf16[128,2048]{1,0:T(8,128)(2,1)}) custom-call(bf16[2,64,128]{2,1,0:T(8,128)(2,1)} %bitcast_bitcast_fusion.2.q_ref, bf16[2,64,256]{2,1,0:T(8,128)(2,1)} %pad_maximum_fusion.kv_ref, ...), custom_call_target="tpu_custom_call" | custom-call | tf_op jit(solution)/shard_map/pallas_call | solution.py:139
  50.7 1.8 %fusion.52 = (f32[128]{0:T(128)S(1)}, f32[128,4096]{1,0:T(8,128)S(1)}) fusion(pred[128,4096]{1,0:T(32,128)(4,1)S(1)} %convolution_compare_fusion, bf16[128,128]{1,0:T(8,128)(2,1)} %bitcast.76, bf16[4096,256]{1,0:T(8,128)(2,1)} %bitcast.73), kind=kOutput, calls=%fused_computation.75 | convolution fusion | flops 135790464 | bytes 3703296 | tf_op jit(solution)/shard_map/qd,kd->qk/dot_general | solution.py:341
  52.5 0.0 copy-start.4
  52.5 0.6 fusion.2
  53.2 0.9 copy-done.4
  54.1 0.0 copy-start.10
  54.1 0.0 copy-start.5
  54.1 1.3 fusion.8
  55.4 0.0 copy-start.9
  55.4 11.0 %shard_map.110 = bf16[8,2,64,128]{3,2,1,0:T(8,128)(2,1)} custom-call(bf16[2,64,128]{2,1,0:T(8,128)(2,1)} %bitcast.77), custom_call_target="tpu_custom_call" | custom-call | tf_op jit(solution)/shard_map/pallas_call | solution.py:194
  66.4 1.1 copy.19
  67.5 0.0 copy-done.10
  67.5 0.2 convert_reduce_fusion
  67.7 0.0 copy-done
  67.7 0.0 copy-done.5
  67.8 1.0 fusion.9.x_ref
  68.8 8.7 %shard_map.111 = bf16[8,8,256]{2,1,0:T(8,128)(2,1)} custom-call(bf16[8,8,256]{2,1,0:T(8,128)(2,1)} %fusion.9.x_ref), custom_call_target="tpu_custom_call" | custom-call | tf_op jit(solution)/shard_map/pallas_call | solution.py:225
  77.4 0.9 multiply_reduce_fusion
  78.3 0.0 copy-done.9
  78.3 1.5 multiply_convert_fusion.x_ref
  79.8 0.0 copy-start.2
  79.8 0.0 copy-start.3
  79.8 32.1 %shard_map.112 = bf16[8,4,8,2048]{3,2,1,0:T(8,128)(2,1)} custom-call(bf16[8,2048]{1,0:T(8,128)(2,1)} %multiply_convert_fusion.x_ref), custom_call_target="tpu_custom_call" | custom-call | tf_op jit(solution)/shard_map/pallas_call | solution.py:154
  111.9 0.0 copy-start.1
  111.9 1.9 %fusion.53 = f32[256,128]{1,0:T(8,128)S(1)} fusion(bf16[256,2048]{1,0:T(8,128)(2,1)} %bitcast.61, bf16[2048,128]{1,0:T(8,128)(2,1)} %get-tuple-element.12), kind=kOutput, calls=%fused_computation.76 | convolution fusion | flops 134217728 | bytes 1703936 | tf_op jit(solution)/shard_map/dot_general | solution.py:372
  113.8 1.8 %fusion.47 = f32[256,128]{1,0:T(8,128)S(1)} fusion(bf16[256,2048]{1,0:T(8,128)(2,1)} %bitcast.62, bf16[1,2048,128]{2,1,0:T(8,128)(2,1)} %param.17), kind=kOutput, calls=%fused_computation.70 | convolution fusion | flops 134217728 | bytes 1703936 | tf_op jit(solution)/shard_map/dot_general | solution.py:372
  115.6 0.0 copy-done.2
  115.6 0.0 copy-done.3
  115.6 0.0 copy-done.1
  115.6 2.1 %fusion.6 = f32[256,2048]{1,0:T(8,128)} fusion(bf16[256,2048]{1,0:T(8,128)(2,1)S(1)} %bitcast.63, f32[256,128]{1,0:T(8,128)S(1)} %fusion.47, bf16[1,128,2048]{2,1,0:T(8,128)(2,1)S(1)} %copy-done.3, bf16[1,2048,128]{2,1,0:T(8,128)(2,1)S(1)} %copy-done.2), kind=kOutput, calls=%fused_computation.12 | convolution fusion | flops 268632064 | bytes 4325376 | tf_op jit(solution)/shard_map/dot_general | solution.py:375
  117.7 3.7 %fusion.1 = bf16[256,2048]{1,0:T(8,128)(2,1)} fusion(f32[256,2048]{1,0:T(8,128)} %fusion.6, bf16[128,2048]{1,0:T(8,128)(2,1)} %get-tuple-element.14, bf16[256,2048]{1,0:T(8,128)(2,1)S(1)} %bitcast.64, bf16[2048,128]{1,0:T(8,128)(2,1)} %get-tuple-element.13, f32[256,128]{1,0:T(8,128)S(1)} %fusion.53), kind=kOutput, calls=%fused_computation.4 | convolution fusion | flops 269680640 | bytes 5373952 | tf_op jit(solution)/shard_map/dot_general | solution.py:375
  121.4 23.4 %shard_map.113 = bf16[8,2048]{1,0:T(8,128)(2,1)} custom-call(bf16[8,4,8,2048]{3,2,1,0:T(8,128)(2,1)} %bitcast.65, bf16[8,2048]{1,0:T(8,128)(2,1)} %bitcast.72), custom_call_target="tpu_custom_call" | custom-call | tf_op jit(solution)/shard_map/pallas_call | solution.py:298
  144.8 1.4 copy.37
  (5 shorter events, 0.0 us)
Async XLA Ops:
  0.0 67.7 %copy-start = (bf16[2048,256]{1,0:T(8,128)(2,1)S(1)}, bf16[2048,256]{1,0:T(8,128)(2,1)}, u32[]{:S(2)}) copy-start(bf16[2048,256]{1,0:T(8,128)(2,1)} %param.15) | copy-start | bytes 3145732
  0.0 1.6 %copy-start.7 = (bf16[64,256]{1,0:T(8,128)(2,1)S(1)}, bf16[64,256]{1,0:T(8,128)(2,1)}, u32[]{:S(2)}) copy-start(bf16[64,256]{1,0:T(8,128)(2,1)} %param.13) | copy-start | bytes 98308
  0.0 1.6 %copy-start.8 = (bf16[64,256]{1,0:T(8,128)(2,1)S(1)}, bf16[64,256]{1,0:T(8,128)(2,1)}, u32[]{:S(2)}) copy-start(bf16[64,256]{1,0:T(8,128)(2,1)} %param.14) | copy-start | bytes 98308
  0.0 2.3 %copy-start.6 = (bf16[64,256]{1,0:T(8,128)(2,1)S(1)}, bf16[64,256]{1,0:T(8,128)(2,1)}, u32[]{:S(2)}) copy-start(bf16[64,256]{1,0:T(8,128)(2,1)} %param.12) | copy-start | bytes 98308
  52.5 1.6 %copy-start.4 = (bf16[8,4,2,64,256]{4,3,2,1,0:T(8,128)(2,1)S(1)}, bf16[8,4,2,64,256]{4,3,2,1,0:T(8,128)(2,1)}, u32[]{:S(2)}) copy-start(bf16[8,4,2,64,256]{4,3,2,1,0:T(8,128)(2,1)} %get-tuple-element.11) | copy-start | bytes 6291460
  54.1 13.4 %copy-start.10 = (s32[64,1]{0,1:T(1,128)S(1)}, s32[64,1]{0,1:T(1,128)}, u32[]{:S(2)}) copy-start(s32[64,1]{0,1:T(1,128)} %param.20) | copy-start | bytes 772
  54.1 13.6 %copy-start.5 = (bf16[64,256]{1,0:T(8,128)(2,1)S(1)}, bf16[64,256]{1,0:T(8,128)(2,1)}, u32[]{:S(2)}) copy-start(bf16[64,256]{1,0:T(8,128)(2,1)} %param.11) | copy-start | bytes 98308
  55.4 22.9 %copy-start.9 = (f32[2048]{0:T(1024)S(1)}, f32[2048]{0:T(1024)}, u32[]{:S(2)}) copy-start(f32[2048]{0:T(1024)} %param.16) | copy-start | bytes 24580
  79.8 35.8 %copy-start.2 = (bf16[1,2048,128]{2,1,0:T(8,128)(2,1)S(1)}, bf16[1,2048,128]{2,1,0:T(8,128)(2,1)}, u32[]{:S(2)}) copy-start(bf16[1,2048,128]{2,1,0:T(8,128)(2,1)} %param.18) | copy-start | bytes 1572868
  79.8 35.8 %copy-start.3 = (bf16[1,128,2048]{2,1,0:T(8,128)(2,1)S(1)}, bf16[1,128,2048]{2,1,0:T(8,128)(2,1)}, u32[]{:S(2)}) copy-start(bf16[1,128,2048]{2,1,0:T(8,128)(2,1)} %param.19) | copy-start | bytes 1572868
  111.9 3.7 %copy-start.1 = (bf16[8,4,8,2048]{3,2,1,0:T(8,128)(2,1)S(1)}, bf16[8,4,8,2048]{3,2,1,0:T(8,128)(2,1)}, u32[]{:S(2)}) copy-start(bf16[8,4,8,2048]{3,2,1,0:T(8,128)(2,1)} %shard_map.112) | copy-start | bytes 3145732

commit v3 on v2

--- a/solution.py
+++ b/solution.py
@@ -35,41 +35,64 @@
     )
 
 
-def spread(nz, ny, at, peer, ref, sems):
+def spread(nz, ny, at, peer, g_ref, large, small, sems):
     z, y, c = at
-    y_send, y_recv, f_send, f_recv, b_send, b_recv = sems
-    up, down = lax.rem(z + 1, nz), lax.rem(z + nz - 1, nz)
+    y_send, y_recv, f_send, f_recv, b_send, b_recv, sz_send, sz_recv, sy_send, sy_recv = sems
+    up, down = peer(lax.rem(z + 1, nz), y, c), peer(lax.rem(z + nz - 1, nz), y, c)
+    half = nz // 2
+    pair = ny // 2
+    far_z = sorted(range(1, nz), key=lambda d: -min(d, nz - d))
+    far_y = sorted(range(1, ny), key=lambda d: -min(d, ny - d))
     pending = []
 
-    def go(copy):
+    def go(ref, send, recv, who):
+        copy = remote(ref, ref, send, recv, who)
         copy.start()
         pending.append(copy)
 
-    for dy in range(1, ny):
-        go(remote(ref(z, y), ref(z, y), y_send.at[dy], y_recv.at[dy], peer(z, lax.rem(y + dy, ny), c)))
-    half = nz // 2
-    events = [(s + j, j, s, d) for j in range(ny) for s in range(half + 1) for d in (1, -1)]
-    for _, j, s, d in sorted(events, key=lambda e: (e[0], e[1], e[2], -e[3])):
-        yy = lax.rem(y + ny - j, ny)
-        longer = 1 if j % 2 == 0 else -1
-        hops = half if d == longer else half - 1
-        if s > hops or (s == 0 and d == -1):
-            continue
-        send, recv = (f_send, f_recv) if d == 1 else (b_send, b_recv)
-        zz = lax.rem(z + nz - d * s, nz)
-        here = ref(zz, yy)
-        if s == 0:
-            if j > 0:
-                remote(here, here, y_send.at[j], y_recv.at[j], peer(z, yy, c)).wait_recv()
-            for d0 in (1, -1):
-                hops0 = half if d0 == longer else half - 1
-                s0, r0 = (f_send, f_recv) if d0 == 1 else (b_send, b_recv)
-                if hops0 > 0:
-                    go(remote(here, here, s0.at[j, 0], r0.at[j, 0], peer(up if d0 == 1 else down, y, c)))
-        else:
-            remote(here, here, send.at[j, s - 1], recv.at[j, s - 1], peer(down if d == 1 else up, y, c)).wait_recv()
-            if s < hops:
-                go(remote(here, here, send.at[j, s], recv.at[j, s], peer(up if d == 1 else down, y, c)))
+    def arrived(ref, send, recv, who):
+        remote(ref, ref, send, recv, who).wait_recv()
+
+    for d in far_y:
+        go(g_ref.at[(z, y) + large], y_send.at[d], y_recv.at[d], peer(z, lax.rem(y + d, ny), c))
+    for d in far_z:
+        go(g_ref.at[(z, y) + small], sz_send.at[d], sz_recv.at[d], peer(lax.rem(z + d, nz), y, c))
+    for d in reversed(far_y):
+        yy = lax.rem(y + ny - d, ny)
+        arrived(g_ref.at[(z, yy) + large], y_send.at[d], y_recv.at[d], peer(z, yy, c))
+
+    def piece(s, k):
+        return g_ref.at[(lax.rem(z + nz + s, nz), pl.ds(k * pair, pair)) + large]
+
+    def onward(s, k):
+        if s < half - 1 or (s == half - 1 and k == 0):
+            go(piece(-s, k), f_send.at[s, k], f_recv.at[s, k], up)
+
+    def backward(s, k):
+        if s < half - 1 or (s == half - 1 and k == 1):
+            go(piece(s, k), b_send.at[s, k], b_recv.at[s, k], down)
+
+    for k in range(2):
+        onward(0, k)
+        backward(0, k)
+    for d in reversed(far_z):
+        zz = lax.rem(z + nz - d, nz)
+        arrived(g_ref.at[(zz, y) + small], sz_send.at[d], sz_recv.at[d], peer(zz, y, c))
+    for d in far_y:
+        ref = g_ref.at[(slice(None), y) + small]
+        go(ref, sy_send.at[d], sy_recv.at[d], peer(z, lax.rem(y + d, ny), c))
+    for s in range(1, half + 1):
+        for k in range(2):
+            if s < half or k == 0:
+                arrived(piece(-s, k), f_send.at[s - 1, k], f_recv.at[s - 1, k], down)
+                onward(s, k)
+            if s < half or k == 1:
+                arrived(piece(s, k), b_send.at[s - 1, k], b_recv.at[s - 1, k], up)
+                backward(s, k)
+    for d in reversed(far_y):
+        yy = lax.rem(y + ny - d, ny)
+        ref = g_ref.at[(slice(None), yy) + small]
+        arrived(ref, sy_send.at[d], sy_recv.at[d], peer(z, yy, c))
     return pending
 
 
@@ -79,9 +102,8 @@
 
 def ring_peers(nz, ny, at, peer):
     z, y, c = at
-    out = [peer(z, lax.rem(y + dy, ny), c) for dy in range(1, ny)]
-    out += [peer(lax.rem(z + 1, nz), y, c), peer(lax.rem(z + nz - 1, nz), y, c)]
-    return out
+    out = [peer(z, lax.rem(y + d, ny), c) for d in range(1, ny)]
+    return out + [peer(lax.rem(z + d, nz), y, c) for d in range(1, nz)]
 
 
 def keys_kernel(
@@ -108,7 +130,10 @@
     ]
     for copy in weights:
         copy.start()
-    pending = spread(nz, ny, at, peer, lambda zz, yy: g_ref.at[zz, yy], sems)
+    cut = g_ref.shape[3] * 3 // 4
+    large = (slice(None), pl.ds(0, cut))
+    small = (slice(None), pl.ds(cut, g_ref.shape[3] - cut))
+    pending = spread(nz, ny, at, peer, g_ref, large, small, sems)
     for copy in pending:
         copy.wait_send()
     for copy in weights:
@@ -127,12 +152,15 @@
     keep.start()
     greet(ring_peers(nz, ny, at, peer))
     keep.wait()
-    for copy in spread(nz, ny, at, peer, lambda zz, yy: g_ref.at[zz, yy], sems):
+    cut = g_ref.shape[3] * 3 // 4
+    large = (slice(None), pl.ds(0, cut))
+    small = (slice(None), pl.ds(cut, g_ref.shape[3] - cut))
+    for copy in spread(nz, ny, at, peer, g_ref, large, small, sems):
         copy.wait_send()
 
 
 def ring_sems(nz, ny):
-    return [DMA((ny,))] * 2 + [DMA((ny, nz))] * 4
+    return [DMA((ny,))] * 2 + [DMA((nz // 2, 2))] * 4 + [DMA((nz,))] * 2 + [DMA((ny,))] * 2
 
 
 def gather_keys(q2, kv2, weights, nz, ny):

time: 147 us -> 135 us (0.918)
  the two profiles are of different devices: /device:TPU:8 before, /device:TPU:2 now
where the time goes in v3:
time: 135 us; the launch traced here: 134 us
  Pallas kernels  111 us (82%)
  matrix products  15.1 us (11%)
  local copies, waits for them, and re-layouts  4.11 us (3%)
  other arithmetic  3.83 us (3%)
    pallas_call x1, Pallas kernels, gather_keys(): pl.pallas_call(functools.partial(keys_kernel, nz, ny), out_shape=(jax.Sha...  42.8 us
    pallas_call x1, Pallas kernels, gather_rows(): pl.pallas_call(functools.partial(rows_kernel, nz, ny), out_shape=jax.Shap...  26.8 us
    pallas_call x1, Pallas kernels, sum_rows(): pl.pallas_call(functools.partial(sum_kernel, nz, ny), out_shape=jax.Shape...  22.8 us
    pallas_call x1, Pallas kernels, share_heads(): pl.pallas_call(functools.partial(heads_kernel, ny, ne), out_shape=jax.Sha...  9.79 us
    pallas_call x1, Pallas kernels, share_pieces(): pl.pallas_call(functools.partial(pieces_kernel, ne), out_shape=jax.ShapeD...  8.53 us
    dot_general x2, matrix products, body(): terms = terms + jnp.dot(activ, down, preferred_element_type=jnp.float32)  5.81 us
    dot_general x2, matrix products, body(): gate_v = jnp.dot(normed_rows, gate, preferred_element_type=jnp.float32)  3.64 us

profile of v3, /device:TPU:2, one launch (start us, length us, event | category | flops | bytes accessed | tf_op | source)
XLA Modules:
  0.0 133.9 jit_solution(8130001112970844240)
XLA Ops:
  0.0 0.0 copy-start
  0.0 0.0 copy-start.7
  0.0 0.0 copy-start.8
  0.0 0.0 copy-start.6
  0.1 1.5 %convolution_compare_fusion = pred[128,4096]{1,0:T(32,128)(4,1)S(1)} fusion(s32[4096]{0:T(1024)S(1)} %add_select_fusion, s32[128]{0:T(128)S(1)} %and_select_fusion, s32[32,32]{1,0:T(8,128)} %param.21), kind=kOutput, calls=%fused_computation.2 | convolution fusion | flops 34477056 | bytes 545280 | tf_op jit(solution)/shard_map/dot_general | solution.py:367
  1.6 0.0 copy-done.7
  1.6 0.0 copy-done.8
  1.6 0.6 pad_maximum_fusion.kv_ref
  2.3 0.0 copy-done.6
  2.3 0.6 bitcast_bitcast_fusion.2.q_ref
  2.9 42.8 %shard_map.109 = (bf16[2,64,128]{2,1,0:T(8,128)(2,1)}, bf16[8,4,2,64,256]{4,3,2,1,0:T(8,128)(2,1)}, bf16[2048,128]{1,0:T(8,128)(2,1)}, bf16[2048,128]{1,0:T(8,128)(2,1)}, bf16[128,2048]{1,0:T(8,128)(2,1)}) custom-call(bf16[2,64,128]{2,1,0:T(8,128)(2,1)} %bitcast_bitcast_fusion.2.q_ref, bf16[2,64,256]{2,1,0:T(8,128)(2,1)} %pad_maximum_fusion.kv_ref, ...), custom_call_target="tpu_custom_call" | custom-call | tf_op jit(solution)/shard_map/pallas_call | solution.py:167
  45.7 1.8 %fusion.52 = (f32[128]{0:T(128)S(1)}, f32[128,4096]{1,0:T(8,128)S(1)}) fusion(pred[128,4096]{1,0:T(32,128)(4,1)S(1)} %convolution_compare_fusion, bf16[128,128]{1,0:T(8,128)(2,1)} %bitcast.76, bf16[4096,256]{1,0:T(8,128)(2,1)} %bitcast.73), kind=kOutput, calls=%fused_computation.75 | convolution fusion | flops 135790464 | bytes 3703296 | tf_op jit(solution)/shard_map/qd,kd->qk/dot_general | solution.py:369
  47.5 0.0 copy-start.4
  47.5 0.6 fusion.2
  48.2 0.9 copy-done.4
  49.1 0.0 copy-start.10
  49.1 0.0 copy-start.5
  49.1 1.3 fusion.8
  50.4 0.0 copy-start.9
  50.4 9.8 %shard_map.110 = bf16[8,2,64,128]{3,2,1,0:T(8,128)(2,1)} custom-call(bf16[2,64,128]{2,1,0:T(8,128)(2,1)} %bitcast.77), custom_call_target="tpu_custom_call" | custom-call | tf_op jit(solution)/shard_map/pallas_call | solution.py:222
  60.2 1.1 copy.19
  61.3 0.0 copy-done.10
  61.3 0.2 convert_reduce_fusion
  61.5 0.0 copy-done
  61.5 0.0 copy-done.5
  61.5 1.0 fusion.9.x_ref
  62.5 8.5 %shard_map.111 = bf16[8,8,256]{2,1,0:T(8,128)(2,1)} custom-call(bf16[8,8,256]{2,1,0:T(8,128)(2,1)} %fusion.9.x_ref), custom_call_target="tpu_custom_call" | custom-call | tf_op jit(solution)/shard_map/pallas_call | solution.py:253
  71.1 0.9 multiply_reduce_fusion
  72.0 0.0 copy-done.9
  72.0 1.5 %multiply_convert_fusion.x_ref = bf16[8,2048]{1,0:T(8,128)(2,1)} fusion(bf16[8,2048]{1,0:T(8,128)(2,1)} %bitcast.71, f32[2048]{0:T(1024)S(1)} %copy-done.9, f32[8]{0:T(128)S(1)} %add_rsqrt_fusion), kind=kLoop, calls=%fused_computation.41 | loop fusion | flops 65536 | bytes 73760 | tf_op jit(solution)/shard_map/convert_element_type | solution.py:396
  73.4 0.0 copy-start.2
  73.4 0.0 copy-start.3
  73.4 26.8 %shard_map.112 = bf16[8,4,8,2048]{3,2,1,0:T(8,128)(2,1)} custom-call(bf16[8,2048]{1,0:T(8,128)(2,1)} %multiply_convert_fusion.x_ref), custom_call_target="tpu_custom_call" | custom-call | tf_op jit(solution)/shard_map/pallas_call | solution.py:182
  100.2 0.0 copy-start.1
  100.2 1.9 %fusion.53 = f32[256,128]{1,0:T(8,128)S(1)} fusion(bf16[256,2048]{1,0:T(8,128)(2,1)} %bitcast.61, bf16[2048,128]{1,0:T(8,128)(2,1)} %get-tuple-element.12), kind=kOutput, calls=%fused_computation.76 | convolution fusion | flops 134217728 | bytes 1703936 | tf_op jit(solution)/shard_map/dot_general | solution.py:400
  102.1 1.8 %fusion.47 = f32[256,128]{1,0:T(8,128)S(1)} fusion(bf16[256,2048]{1,0:T(8,128)(2,1)} %bitcast.62, bf16[1,2048,128]{2,1,0:T(8,128)(2,1)} %param.17), kind=kOutput, calls=%fused_computation.70 | convolution fusion | flops 134217728 | bytes 1703936 | tf_op jit(solution)/shard_map/dot_general | solution.py:400
  103.9 0.0 copy-done.2
  103.9 0.0 copy-done.3
  103.9 0.0 copy-done.1
  103.9 2.1 %fusion.6 = f32[256,2048]{1,0:T(8,128)} fusion(bf16[256,2048]{1,0:T(8,128)(2,1)S(1)} %bitcast.63, f32[256,128]{1,0:T(8,128)S(1)} %fusion.47, bf16[1,128,2048]{2,1,0:T(8,128)(2,1)S(1)} %copy-done.3, bf16[1,2048,128]{2,1,0:T(8,128)(2,1)S(1)} %copy-done.2), kind=kOutput, calls=%fused_computation.12 | convolution fusion | flops 268632064 | bytes 4325376 | tf_op jit(solution)/shard_map/dot_general | solution.py:403
  106.0 3.7 %fusion.1 = bf16[256,2048]{1,0:T(8,128)(2,1)} fusion(f32[256,2048]{1,0:T(8,128)} %fusion.6, bf16[128,2048]{1,0:T(8,128)(2,1)} %get-tuple-element.14, bf16[256,2048]{1,0:T(8,128)(2,1)S(1)} %bitcast.64, bf16[2048,128]{1,0:T(8,128)(2,1)} %get-tuple-element.13, f32[256,128]{1,0:T(8,128)S(1)} %fusion.53), kind=kOutput, calls=%fused_computation.4 | convolution fusion | flops 269680640 | bytes 5373952 | tf_op jit(solution)/shard_map/dot_general | solution.py:403
  109.7 22.8 %shard_map.113 = bf16[8,2048]{1,0:T(8,128)(2,1)} custom-call(bf16[8,4,8,2048]{3,2,1,0:T(8,128)(2,1)} %bitcast.65, bf16[8,2048]{1,0:T(8,128)(2,1)} %bitcast.72), custom_call_target="tpu_custom_call" | custom-call | tf_op jit(solution)/shard_map/pallas_call | solution.py:326
  132.5 1.4 %copy.37 = bf16[1,8,2048]{2,1,0:T(8,128)(2,1)} copy(bf16[1,8,2048]{2,1,0:T(8,128)(2,1)} %bitcast.75) | data formatting | bytes 65536
  (5 shorter events, 0.0 us)
Async XLA Ops:
  0.0 61.5 %copy-start = (bf16[2048,256]{1,0:T(8,128)(2,1)S(1)}, bf16[2048,256]{1,0:T(8,128)(2,1)}, u32[]{:S(2)}) copy-start(bf16[2048,256]{1,0:T(8,128)(2,1)} %param.15) | copy-start | bytes 3145732
  0.0 1.6 %copy-start.7 = (bf16[64,256]{1,0:T(8,128)(2,1)S(1)}, bf16[64,256]{1,0:T(8,128)(2,1)}, u32[]{:S(2)}) copy-start(bf16[64,256]{1,0:T(8,128)(2,1)} %param.13) | copy-start | bytes 98308
  0.0 1.6 %copy-start.8 = (bf16[64,256]{1,0:T(8,128)(2,1)S(1)}, bf16[64,256]{1,0:T(8,128)(2,1)}, u32[]{:S(2)}) copy-start(bf16[64,256]{1,0:T(8,128)(2,1)} %param.14) | copy-start | bytes 98308
  0.0 2.2 %copy-start.6 = (bf16[64,256]{1,0:T(8,128)(2,1)S(1)}, bf16[64,256]{1,0:T(8,128)(2,1)}, u32[]{:S(2)}) copy-start(bf16[64,256]{1,0:T(8,128)(2,1)} %param.12) | copy-start | bytes 98308
  47.5 1.6 %copy-start.4 = (bf16[8,4,2,64,256]{4,3,2,1,0:T(8,128)(2,1)S(1)}, bf16[8,4,2,64,256]{4,3,2,1,0:T(8,128)(2,1)}, u32[]{:S(2)}) copy-start(bf16[8,4,2,64,256]{4,3,2,1,0:T(8,128)(2,1)} %get-tuple-element.11) | copy-start | bytes 6291460
  49.1 12.2 %copy-start.10 = (s32[64,1]{0,1:T(1,128)S(1)}, s32[64,1]{0,1:T(1,128)}, u32[]{:S(2)}) copy-start(s32[64,1]{0,1:T(1,128)} %param.20) | copy-start | bytes 772
  49.1 12.4 %copy-start.5 = (bf16[64,256]{1,0:T(8,128)(2,1)S(1)}, bf16[64,256]{1,0:T(8,128)(2,1)}, u32[]{:S(2)}) copy-start(bf16[64,256]{1,0:T(8,128)(2,1)} %param.11) | copy-start | bytes 98308
  50.4 21.6 %copy-start.9 = (f32[2048]{0:T(1024)S(1)}, f32[2048]{0:T(1024)}, u32[]{:S(2)}) copy-start(f32[2048]{0:T(1024)} %param.16) | copy-start | bytes 24580
  73.4 30.4 %copy-start.2 = (bf16[1,2048,128]{2,1,0:T(8,128)(2,1)S(1)}, bf16[1,2048,128]{2,1,0:T(8,128)(2,1)}, u32[]{:S(2)}) copy-start(bf16[1,2048,128]{2,1,0:T(8,128)(2,1)} %param.18) | copy-start | bytes 1572868
  73.4 30.4 %copy-start.3 = (bf16[1,128,2048]{2,1,0:T(8,128)(2,1)S(1)}, bf16[1,128,2048]{2,1,0:T(8,128)(2,1)}, u32[]{:S(2)}) copy-start(bf16[1,128,2048]{2,1,0:T(8,128)(2,1)} %param.19) | copy-start | bytes 1572868
  100.2 3.7 %copy-start.1 = (bf16[8,4,8,2048]{3,2,1,0:T(8,128)(2,1)S(1)}, bf16[8,4,8,2048]{3,2,1,0:T(8,128)(2,1)}, u32[]{:S(2)}) copy-start(bf16[8,4,8,2048]{3,2,1,0:T(8,128)(2,1)} %shard_map.112) | copy-start | bytes 3145732

commit v4 on v3

--- a/solution.py
+++ b/solution.py
@@ -145,20 +145,6 @@
     swap_q.wait_send()
 
 
-def rows_kernel(nz, ny, x_ref, g_ref, own, *sems):
-    at = z, y, c = place(ny)
-    peer = ctx_peer(ny)
-    keep = pltpu.make_async_copy(x_ref, g_ref.at[z, y], own)
-    keep.start()
-    greet(ring_peers(nz, ny, at, peer))
-    keep.wait()
-    cut = g_ref.shape[3] * 3 // 4
-    large = (slice(None), pl.ds(0, cut))
-    small = (slice(None), pl.ds(cut, g_ref.shape[3] - cut))
-    for copy in spread(nz, ny, at, peer, g_ref, large, small, sems):
-        copy.wait_send()
-
-
 def ring_sems(nz, ny):
     return [DMA((ny,))] * 2 + [DMA((nz // 2, 2))] * 4 + [DMA((nz,))] * 2 + [DMA((ny,))] * 2
 
@@ -178,62 +164,30 @@
     )(q2, kv2, *weights)
 
 
-def gather_rows(x, nz, ny):
-    return pl.pallas_call(
-        functools.partial(rows_kernel, nz, ny),
-        out_shape=jax.ShapeDtypeStruct((nz, ny) + x.shape, x.dtype),
-        in_specs=[VM],
-        out_specs=VM,
-        scratch_shapes=[DMA] + ring_sems(nz, ny),
-        compiler_params=pltpu.CompilerParams(collective_id=1, has_side_effects=True),
-    )(x)
-
-
-def heads_kernel(ny, ne, a_ref, o_ref, own, send, recv):
+def swap_heads(ny, ne, a_ref, o_ref, own, send, recv):
     z, y, c = place(ny)
     e = lax.axis_index("exp")
-
-    def peer(de, dc):
-        return {
-            "ctx": (z * ny + y) * 2 + lax.rem(c + dc, 2),
-            "exp": lax.rem(e + de, ne),
-        }
-
-    others = [(de, dc) for de in range(ne) for dc in range(2) if de or dc]
     keep = pltpu.make_async_copy(a_ref.at[c], o_ref.at[e, c], own)
     keep.start()
-    greet([peer(de, dc) for de, dc in others])
+    others = [(de, dc) for de in range(ne) for dc in range(2) if de or dc]
     copies = []
     for de, dc in others:
-        copy = remote(
-            a_ref.at[lax.rem(c + dc, 2)], o_ref.at[e, c], send.at[de, dc], recv.at[de, dc], peer(de, dc)
-        )
+        to = {"ctx": (z * ny + y) * 2 + lax.rem(c + dc, 2), "exp": lax.rem(e + de, ne)}
+        copy = remote(a_ref.at[lax.rem(c + dc, 2)], o_ref.at[e, c], send.at[de, dc], recv.at[de, dc], to)
         copy.start()
         copies.append(copy)
     keep.wait()
     for de, dc in others:
-        got = o_ref.at[lax.rem(e + ne - de, ne), lax.rem(c + dc, 2)]
-        remote(got, got, send.at[de, dc], recv.at[de, dc], peer(de, dc)).wait_recv()
-    for copy in copies:
-        copy.wait_send()
-
-
-def share_heads(a, ny, ne):
-    return pl.pallas_call(
-        functools.partial(heads_kernel, ny, ne),
-        out_shape=jax.ShapeDtypeStruct((ne,) + a.shape, a.dtype),
-        in_specs=[VM],
-        out_specs=VM,
-        scratch_shapes=[DMA, DMA((ne, 2)), DMA((ne, 2))],
-        compiler_params=pltpu.CompilerParams(collective_id=2, has_side_effects=True),
-    )(a)
-
-
-def pieces_kernel(ne, x_ref, o_ref, own, send, recv):
+        back = lax.rem(e + ne - de, ne)
+        got = o_ref.at[back, lax.rem(c + dc, 2)]
+        remote(got, got, send.at[de, dc], recv.at[de, dc], {"exp": back}).wait_recv()
+    return copies
+
+
+def swap_pieces(ne, x_ref, o_ref, own, send, recv):
     e = lax.axis_index("exp")
     keep = pltpu.make_async_copy(x_ref.at[e], o_ref.at[e], own)
     keep.start()
-    greet([{"exp": lax.rem(e + de, ne)} for de in range(1, ne)])
     copies = []
     for de in range(1, ne):
         to = lax.rem(e + de, ne)
@@ -245,22 +199,10 @@
         back = lax.rem(e + ne - de, ne)
         got = o_ref.at[back]
         remote(got, got, send.at[de], recv.at[de], {"exp": back}).wait_recv()
-    for copy in copies:
-        copy.wait_send()
-
-
-def share_pieces(x, ne):
-    return pl.pallas_call(
-        functools.partial(pieces_kernel, ne),
-        out_shape=jax.ShapeDtypeStruct(x.shape, x.dtype),
-        in_specs=[VM],
-        out_specs=VM,
-        scratch_shapes=[DMA, DMA((ne,)), DMA((ne,))],
-        compiler_params=pltpu.CompilerParams(collective_id=4, has_side_effects=True),
-    )(x)
-
-
-def sum_kernel(nz, ny, t_ref, h_ref, o_ref, rz, ry, uz, uy, vz, vy, *sems):
+    return copies
+
+
+def sum_rows(nz, ny, t_ref, own_rows, o_ref, rz, ry, uz, uy, vz, vy, sems):
     z, y, c = place(ny)
     rz_send, rz_recv, ry_send, ry_recv, vz_send, vz_recv, vy_send, vy_recv = sems
     half = t_ref.shape[-1] // 2
@@ -270,7 +212,6 @@
     far_y = sorted(range(1, ny), key=lambda d: -min(d, ny - d))
     to_z = {d: lax.rem(z + d, nz) for d in far_z}
     to_y = {d: lax.rem(y + d, ny) for d in far_y}
-    greet([peer(to_z[d], y, c) for d in far_z] + [peer(z, to_y[d], c) for d in far_y])
 
     def send(src, dst, sends, recvs, who):
         copy = remote(src, dst, sends, recvs, who)
@@ -301,37 +242,132 @@
     then_z = [
         send(uy.at[to_z[d]], vy.at[d], vy_send.at[d], vy_recv.at[d], peer(to_z[d], y, c)) for d in far_z
     ]
-    result = h_ref[:, :half].astype(jnp.float32) + uz[y].astype(jnp.float32)
+    result = own_rows[:, :half] + uz[y].astype(jnp.float32)
     for d, copy in zip(far_y, then_y):
         copy.wait_recv()
         result = result + vz[d].astype(jnp.float32)
     o_ref[:, :half] = result.astype(jnp.bfloat16)
-    result = h_ref[:, half:].astype(jnp.float32) + uy[z].astype(jnp.float32)
+    result = own_rows[:, half:] + uy[z].astype(jnp.float32)
     for d, copy in zip(far_z, then_z):
         copy.wait_recv()
         result = result + vy[d].astype(jnp.float32)
     o_ref[:, half:] = result.astype(jnp.bfloat16)
-    for copy in by_z + by_y + then_y + then_z:
+    return by_z + by_y + then_y + then_z
+
+
+def layer_kernel(
+    nz, ny, ne, a_ref, res_ref, proj_ref, place_ref, gain_ref, w0, w1, w2, p0, p1, p2, o_ref,
+    heads, pieces, own, g_buf, rows_buf, t_buf, b0, b1, b2, c0, c1, c2,
+    rz, ry, uz, uy, vz, vy, local, h_send, h_recv, p_send, p_recv, *sems
+):
+    at = z, y, c = place(ny)
+    e = lax.axis_index("exp")
+    peer = ctx_peer(ny)
+    loads = [
+        pltpu.make_async_copy(src, dst, local.at[2 + i])
+        for i, (src, dst) in enumerate(
+            [(w0, b0), (w1, b1), (w2, b2), (p0, c0), (p1, c1), (p2, c2)]
+        )
+    ]
+    for copy in loads:
+        copy.start()
+    greet(
+        ring_peers(nz, ny, at, peer)
+        + [
+            {"ctx": (z * ny + y) * 2 + lax.rem(c + dc, 2), "exp": lax.rem(e + de, ne)}
+            for de in range(ne)
+            for dc in range(2)
+            if de or dc
+        ]
+    )
+    sent = swap_heads(ny, ne, a_ref, heads, local.at[0], h_send, h_recv)
+    hidden = res_ref[...].astype(jnp.float32)
+    for i in range(ne):
+        for j in range(2):
+            h = 2 * i + j
+            hidden = hidden + jnp.dot(
+                heads[i, j], proj_ref[h * HD : (h + 1) * HD, :], preferred_element_type=jnp.float32
+            )
+    hidden = hidden.astype(jnp.bfloat16)
+    slots = jnp.dot(place_ref[...], hidden, preferred_element_type=jnp.float32)
+    pieces[...] = slots.reshape(pieces.shape).astype(jnp.bfloat16)
+    sent += swap_pieces(ne, pieces, own, local.at[1], p_send, p_recv)
+    part = own.shape[2]
+    width = ne * part
+    own_f = [own[i].astype(jnp.float32) for i in range(ne)]
+    square = own_f[0] * own_f[0]
+    for v in own_f[1:]:
+        square = square + v * v
+    inv = lax.rsqrt(jnp.sum(square, axis=1, keepdims=True) / width + 1e-05)
+    for i, v in enumerate(own_f):
+        cols = slice(i * part, (i + 1) * part)
+        g_buf[z, y, :, cols] = (v * inv * gain_ref[:, cols]).astype(jnp.bfloat16)
+    cut = width * 3 // 4
+    large = (slice(None), pl.ds(0, cut))
+    small = (slice(None), pl.ds(cut, width - cut))
+    sent += spread(nz, ny, at, peer, g_buf, large, small, sems[:10])
+    count = rows_buf.shape[0]
+    rows_buf[...] = g_buf[...].astype(jnp.float32).reshape(count, width).astype(jnp.bfloat16)
+    for copy in loads:
+        copy.wait()
+    rows = rows_buf[...]
+    acts = []
+    for gate, up in ((b0, b1), (c0, c1)):
+        gate_v = jnp.dot(rows, gate[...], preferred_element_type=jnp.float32)
+        up_v = jnp.dot(rows, up[...], preferred_element_type=jnp.float32)
+        acts.append((gate_v / (1.0 + jnp.exp(-gate_v)) * up_v).astype(jnp.bfloat16))
+    step = width // 4
+    for i in range(4):
+        cols = slice(i * step, (i + 1) * step)
+        terms = jnp.dot(acts[0], b2[:, cols], preferred_element_type=jnp.float32)
+        terms = terms + jnp.dot(acts[1], c2[:, cols], preferred_element_type=jnp.float32)
+        t_buf[:, :, :, cols] = terms.reshape(t_buf.shape[:3] + (step,)).astype(jnp.bfloat16)
+    own_rows = jnp.concatenate([own[i].astype(jnp.float32) for i in range(ne)], axis=1)
+    sent += sum_rows(nz, ny, t_buf, own_rows, o_ref, rz, ry, uz, uy, vz, vy, sems[10:])
+    for copy in sent:
         copy.wait_send()
 
 
-def sum_rows(terms, own, nz, ny):
-    rows, width = own.shape
+def rest(attended, residual, out_proj, placing, gain, mine, partner, nz, ny, ne):
+    tokens, part = residual.shape
+    rows, width = tokens // ne, ne * part
     half = width // 2
-    t = terms.reshape(nz, ny, rows, width)
-
-    def buf(*lead):
-        return pltpu.VMEM(lead + (rows, half), jnp.bfloat16)
-
+    units = mine[0].shape[1]
+
+    def buf(*shape):
+        return pltpu.VMEM(shape, jnp.bfloat16)
+
+    weights = [buf(width, units), buf(width, units), buf(units, width)]
     return pl.pallas_call(
-        functools.partial(sum_kernel, nz, ny),
-        out_shape=jax.ShapeDtypeStruct(own.shape, own.dtype),
-        in_specs=[VM, VM],
+        functools.partial(layer_kernel, nz, ny, ne),
+        out_shape=jax.ShapeDtypeStruct((rows, width), jnp.bfloat16),
+        in_specs=[VM] * 5 + [ANY] * 6,
         out_specs=VM,
-        scratch_shapes=[buf(nz, ny), buf(ny, nz), buf(ny), buf(nz), buf(ny), buf(nz)]
-        + [DMA((n,)) for n in (nz, nz, ny, ny, ny, ny, nz, nz)],
-        compiler_params=pltpu.CompilerParams(collective_id=3, has_side_effects=True),
-    )(t, own)
+        scratch_shapes=[
+            buf(ne, 2, tokens, HD),
+            buf(ne, rows, part),
+            buf(ne, rows, part),
+            buf(nz, ny, rows, width),
+            buf(nz * ny * rows, width),
+            buf(nz, ny, rows, width),
+            *weights,
+            *weights,
+            buf(nz, ny, rows, half),
+            buf(ny, nz, rows, half),
+            buf(ny, rows, half),
+            buf(nz, rows, half),
+            buf(ny, rows, half),
+            buf(nz, rows, half),
+            DMA((8,)),
+            DMA((ne, 2)),
+            DMA((ne, 2)),
+            DMA((ne,)),
+            DMA((ne,)),
+            *ring_sems(nz, ny),
+            *(DMA((n,)) for n in (nz, nz, ny, ny, ny, ny, nz, nz)),
+        ],
+        compiler_params=pltpu.CompilerParams(collective_id=1, has_side_effects=True),
+    )(attended, residual, out_proj, placing, gain, *mine, *partner)
 
 
 def body(
@@ -376,11 +412,6 @@
         exponent.astype(jnp.bfloat16), kv_all[:, HD:], preferred_element_type=jnp.float32
     )
     attended = (product / total).astype(jnp.bfloat16).reshape(2, local_tokens, HD)
-    heads = share_heads(attended, ny, expert_count)
-    heads = heads.reshape(2 * expert_count, local_tokens, HD)
-    heads = heads.transpose(1, 0, 2).reshape(local_tokens, 2 * expert_count * HD)
-    projected = jnp.dot(heads, out_proj, preferred_element_type=jnp.float32)
-    hidden = (residual.astype(jnp.float32) + projected).astype(jnp.bfloat16)
     target = routes[:, 0]
     token_ids = jnp.arange(local_tokens, dtype=jnp.int32)
     earlier = (target[:, None] == target[None, :]) & (token_ids[None, :] < token_ids[:, None])
@@ -388,21 +419,9 @@
     slot_of = target * per_expert + ranking
     slot_ids = jnp.arange(expert_count * per_expert, dtype=jnp.int32)
     placing = (slot_of[None, :] == slot_ids[:, None]).astype(jnp.bfloat16)
-    send_buffer = jnp.dot(placing, hidden, preferred_element_type=jnp.float32).astype(jnp.bfloat16)
-    send_buffer = send_buffer.reshape(expert_count, per_expert, hidden.shape[1])
-    own_rows = share_pieces(send_buffer, expert_count).transpose(1, 0, 2).reshape(per_expert, -1)
-    values_f = own_rows.astype(jnp.float32)
-    meansq = jnp.mean(values_f * values_f, axis=1, keepdims=True)
-    normed_own = (values_f * lax.rsqrt(meansq + 1e-05) * norm_gain).astype(jnp.bfloat16)
-    normed_rows = gather_rows(normed_own, nz, ny).reshape(-1, normed_own.shape[1])
-    terms = 0.0
-    for gate, up, down in (mine, partner):
-        gate_v = jnp.dot(normed_rows, gate, preferred_element_type=jnp.float32)
-        up_v = jnp.dot(normed_rows, up, preferred_element_type=jnp.float32)
-        activ = (jax.nn.silu(gate_v) * up_v).astype(jnp.bfloat16)
-        terms = terms + jnp.dot(activ, down, preferred_element_type=jnp.float32)
-    terms = terms.astype(jnp.bfloat16)
-    return sum_rows(terms, own_rows, nz, ny)[None]
+    return rest(
+        attended, residual, out_proj, placing, norm_gain[None], mine, partner, nz, ny, expert_count
+    )[None]
 
 
 def solution(mesh):

time: 135 us -> 111 us (0.82)
  the two profiles are of different devices: /device:TPU:2 before, /device:TPU:8 now
where the time goes in v4:
time: 111 us; the launch traced here: 110 us
  Pallas kernels  101 us (91%)
  matrix products  4.54 us (4%)
  local copies, waits for them, and re-layouts  2.96 us (3%)
  other arithmetic  2.09 us (2%)
    pallas_call x1, Pallas kernels, rest(): pl.pallas_call(functools.partial(layer_kernel, nz, ny, ne), out_shape=jax...  58.7 us
    pallas_call x1, Pallas kernels, gather_keys(): pl.pallas_call(functools.partial(keys_kernel, nz, ny), out_shape=(jax.Sha...  42.1 us
    unnamed x11, local copies, waits for them, and re-layouts  2.33 us

profile of v4, /device:TPU:8, one launch (start us, length us, event | category | flops | bytes accessed | tf_op | source)
XLA Modules:
  0.0 110.5 jit_solution(7646484432856983397)
XLA Ops:
  0.0 0.0 copy-start
  0.0 0.0 copy-start.3
  0.0 0.0 copy-start.2
  0.1 1.4 %convolution_compare_fusion = pred[128,4096]{1,0:T(32,128)(4,1)S(1)} fusion(s32[4096]{0:T(1024)S(1)} %add_select_fusion, s32[128]{0:T(128)S(1)} %and_select_fusion, s32[32,32]{1,0:T(8,128)} %param.21), kind=kOutput, calls=%fused_computation.2 | convolution fusion | flops 34477056 | bytes 545280 | tf_op jit(solution)/shard_map/dot_general | solution.py:403
  1.5 0.0 copy-done
  1.5 0.0 copy-done.3
  1.5 0.6 pad_maximum_fusion.kv_ref
  2.2 0.0 copy-done.2
  2.2 0.6 bitcast_bitcast_fusion.2.q_ref
  2.8 42.1 %shard_map.109 = (bf16[2,64,128]{2,1,0:T(8,128)(2,1)}, bf16[8,4,2,64,256]{4,3,2,1,0:T(8,128)(2,1)}, bf16[2048,128]{1,0:T(8,128)(2,1)}, bf16[2048,128]{1,0:T(8,128)(2,1)}, bf16[128,2048]{1,0:T(8,128)(2,1)}) custom-call(bf16[2,64,128]{2,1,0:T(8,128)(2,1)} %bitcast_bitcast_fusion.2.q_ref, bf16[2,64,256]{2,1,0:T(8,128)(2,1)} %pad_maximum_fusion.kv_ref, ...), custom_call_target="tpu_custom_call" | custom-call | tf_op jit(solution)/shard_map/pallas_call | solution.py:153
  44.9 1.8 %fusion.22 = (f32[128]{0:T(128)S(1)}, f32[128,4096]{1,0:T(8,128)S(1)}) fusion(pred[128,4096]{1,0:T(32,128)(4,1)S(1)} %convolution_compare_fusion, bf16[128,128]{1,0:T(8,128)(2,1)} %bitcast.42, bf16[4096,256]{1,0:T(8,128)(2,1)} %bitcast.38), kind=kOutput, calls=%fused_computation.40 | convolution fusion | flops 135790464 | bytes 3703296 | tf_op jit(solution)/shard_map/qd,kd->qk/dot_general | solution.py:405
  46.7 0.0 copy-start.1
  46.7 0.6 fusion.1
  47.4 0.9 copy-done.1
  48.3 0.0 copy-start.4
  48.3 1.3 %fusion.3 = bf16[128,128]{1,0:T(8,128)(2,1)} fusion(pred[128,4096]{1,0:T(32,128)(4,1)S(1)} %convolution_compare_fusion, f32[128,4096]{1,0:T(8,128)S(1)} %get-tuple-element.16, bf16[4096,256]{1,0:T(8,128)(2,1)S(1)} %bitcast.39, f32[128]{0:T(128)S(1)} %get-tuple-element.15, f32[128]{0:T(128)S(1)} %fusion.1), kind=kOutput, calls=%fused_computation.7 | convolution fusion | flops 135823360 | bytes 3703808 | tf_op jit(solution)/shard_map/dot_general | solution.py:411
  49.6 0.0 copy-done.4
  49.6 0.2 convert_reduce_fusion
  49.8 0.6 fusion.15.place_ref
  50.4 58.7 %shard_map.110 = bf16[8,2048]{1,0:T(8,128)(2,1)} custom-call(bf16[2,64,128]{2,1,0:T(8,128)(2,1)} %bitcast.41, bf16[64,256]{1,0:T(8,128)(2,1)} %res_ref.1, bf16[2048,256]{1,0:T(8,128)(2,1)} %proj_ref.1, bf16[64,64]{1,0:T(8,128)(2,1)} %fusion.15.place_ref, f32[1,2048]{1,0:T(1,128)} %bitcast.43, bf16[2048,128]{1,0:T(8,128)(2,1)} %bitcast.33, ...), custom_call_target="tpu_custom_call" | custom-call | tf_op jit(solution)/shard_map/pallas_call | solution.py:341
  109.1 1.4 %copy.29 = bf16[1,8,2048]{2,1,0:T(8,128)(2,1)} copy(bf16[1,8,2048]{2,1,0:T(8,128)(2,1)} %bitcast.40) | data formatting | bytes 65536
  (4 shorter events, 0.0 us)
Async XLA Ops:
  0.0 1.5 %copy-start = (bf16[64,256]{1,0:T(8,128)(2,1)S(1)}, bf16[64,256]{1,0:T(8,128)(2,1)}, u32[]{:S(2)}) copy-start(bf16[64,256]{1,0:T(8,128)(2,1)} %param.13) | copy-start | bytes 98308
  0.0 1.5 %copy-start.3 = (bf16[64,256]{1,0:T(8,128)(2,1)S(1)}, bf16[64,256]{1,0:T(8,128)(2,1)}, u32[]{:S(2)}) copy-start(bf16[64,256]{1,0:T(8,128)(2,1)} %param.14) | copy-start | bytes 98308
  0.0 2.1 %copy-start.2 = (bf16[64,256]{1,0:T(8,128)(2,1)S(1)}, bf16[64,256]{1,0:T(8,128)(2,1)}, u32[]{:S(2)}) copy-start(bf16[64,256]{1,0:T(8,128)(2,1)} %param.12) | copy-start | bytes 98308
  46.7 1.6 %copy-start.1 = (bf16[8,4,2,64,256]{4,3,2,1,0:T(8,128)(2,1)S(1)}, bf16[8,4,2,64,256]{4,3,2,1,0:T(8,128)(2,1)}, u32[]{:S(2)}) copy-start(bf16[8,4,2,64,256]{4,3,2,1,0:T(8,128)(2,1)} %get-tuple-element.11) | copy-start | bytes 6291460
  48.3 1.3 %copy-start.4 = (s32[64,1]{0,1:T(1,128)S(1)}, s32[64,1]{0,1:T(1,128)}, u32[]{:S(2)}) copy-start(s32[64,1]{0,1:T(1,128)} %param.20) | copy-start | bytes 772

commit v5 on v4

--- a/solution.py
+++ b/solution.py
@@ -106,62 +106,66 @@
     return out + [peer(lax.rem(z + d, nz), y, c) for d in range(1, nz)]
 
 
-def keys_kernel(
-    nz, ny, q_ref, kv_ref, w0, w1, w2, qo_ref, g_ref, p0, p1, p2, own, d_send, d_recv, *sems
-):
-    at = z, y, c = place(ny)
-    peer = ctx_peer(ny)
-    other = peer(z, y, 1 - c)
-    greet(ring_peers(nz, ny, at, peer) + [other])
-    swap_kv = remote(kv_ref.at[1 - c], g_ref.at[z, y, c], d_send.at[0], d_recv.at[0], other)
-    swap_q = remote(q_ref.at[1 - c], qo_ref.at[c], d_send.at[1], d_recv.at[1], other)
-    swap_kv.start()
-    swap_q.start()
-    keep_kv = pltpu.make_async_copy(kv_ref.at[c], g_ref.at[z, y, c], own.at[0])
-    keep_q = pltpu.make_async_copy(q_ref.at[c], qo_ref.at[c], own.at[1])
-    keep_kv.start()
-    keep_q.start()
-    keep_kv.wait()
-    got = g_ref.at[z, y, 1 - c]
-    remote(got, got, d_send.at[0], d_recv.at[0], other).wait_recv()
-    weights = [
-        remote(src, dst, d_send.at[2 + i], d_recv.at[2 + i], other)
-        for i, (src, dst) in enumerate([(w0, p0), (w1, p1), (w2, p2)])
-    ]
-    for copy in weights:
-        copy.start()
-    cut = g_ref.shape[3] * 3 // 4
-    large = (slice(None), pl.ds(0, cut))
-    small = (slice(None), pl.ds(cut, g_ref.shape[3] - cut))
-    pending = spread(nz, ny, at, peer, g_ref, large, small, sems)
-    for copy in pending:
-        copy.wait_send()
-    for copy in weights:
+def swap_tokens(nz, ny, inputs, q_buf, kv_buf, weights, send, recv, own):
+    z, y, c = place(ny)
+    other = ctx_peer(ny)(z, y, 1 - c)
+    mine = pl.ds(pl.multiple_of(c * HD, HD), HD)
+    theirs = pl.ds(pl.multiple_of((1 - c) * HD, HD), HD)
+    spots = [
+        lambda t: q_buf.at[t],
+        lambda t: kv_buf.at[z, y, t, :, pl.ds(0, HD)],
+        lambda t: kv_buf.at[z, y, t, :, pl.ds(HD, HD)],
+    ]
+    sent, kept = [], []
+    for i, (x, spot) in enumerate(zip(inputs, spots)):
+        copy = remote(x.at[:, theirs], spot(c), send.at[i], recv.at[i], other)
+        copy.start()
+        sent.append(copy)
+        copy = pltpu.make_async_copy(x.at[:, mine], spot(c), own.at[i])
+        copy.start()
+        kept.append(copy)
+    for copy in kept:
         copy.wait()
-    keep_q.wait()
-    got_q = qo_ref.at[1 - c]
-    remote(got_q, got_q, d_send.at[1], d_recv.at[1], other).wait_recv()
-    swap_kv.wait_send()
-    swap_q.wait_send()
+    for i, spot in enumerate(spots):
+        got = spot(1 - c)
+        remote(got, got, send.at[i], recv.at[i], other).wait_recv()
+    swaps = [
+        remote(src, dst, send.at[3 + i], recv.at[3 + i], other) for i, (src, dst) in enumerate(weights)
+    ]
+    for copy in swaps:
+        copy.start()
+    return sent, swaps
+
+
+def attend(nz, q_buf, kv_buf, mask_ref, s_buf, a_buf):
+    tokens = q_buf.shape[0] * q_buf.shape[1]
+    queries = q_buf[...].reshape(tokens, HD)
+    span = s_buf.shape[1] // nz
+    top = jnp.full((tokens, 1), -1e30, jnp.float32)
+    for i in range(nz):
+        cols = slice(i * span, (i + 1) * span)
+        keys = kv_buf[i, :, :, :, :HD].reshape(span, HD)
+        scores = lax.dot_general(
+            queries, keys, (((1,), (1,)), ((), ())), preferred_element_type=jnp.float32
+        ) * (1.0 / math.sqrt(HD))
+        scores = jnp.where(mask_ref[:, cols] > 0, scores, -1e30)
+        s_buf[:, cols] = scores
+        top = jnp.maximum(top, jnp.max(scores, axis=1, keepdims=True))
+    total = jnp.zeros((tokens, 1), jnp.float32)
+    product = jnp.zeros((tokens, HD), jnp.float32)
+    for i in range(nz):
+        cols = slice(i * span, (i + 1) * span)
+        values = kv_buf[i, :, :, :, HD:].reshape(span, HD)
+        expo = jnp.where(mask_ref[:, cols] > 0, jnp.exp(s_buf[:, cols] - top), 0.0)
+        total = total + jnp.sum(expo, axis=1, keepdims=True)
+        product = product + jnp.dot(
+            expo.astype(jnp.bfloat16), values, preferred_element_type=jnp.float32
+        )
+    a_buf[...] = (product / total).astype(jnp.bfloat16).reshape(a_buf.shape)
 
 
 def ring_sems(nz, ny):
     return [DMA((ny,))] * 2 + [DMA((nz // 2, 2))] * 4 + [DMA((nz,))] * 2 + [DMA((ny,))] * 2
-
-
-def gather_keys(q2, kv2, weights, nz, ny):
-    return pl.pallas_call(
-        functools.partial(keys_kernel, nz, ny),
-        out_shape=(
-            jax.ShapeDtypeStruct(q2.shape, q2.dtype),
-            jax.ShapeDtypeStruct((nz, ny) + kv2.shape, kv2.dtype),
-            *(jax.ShapeDtypeStruct(w.shape, w.dtype) for w in weights),
-        ),
-        in_specs=[VM, VM, ANY, ANY, ANY],
-        out_specs=(VM, VM, ANY, ANY, ANY),
-        scratch_shapes=[DMA((2,)), DMA((5,)), DMA((5,))] + ring_sems(nz, ny),
-        compiler_params=pltpu.CompilerParams(collective_id=0, has_side_effects=True),
-    )(q2, kv2, *weights)
 
 
 def swap_heads(ny, ne, a_ref, o_ref, own, send, recv):
@@ -256,9 +260,9 @@
 
 
 def layer_kernel(
-    nz, ny, ne, a_ref, res_ref, proj_ref, place_ref, gain_ref, w0, w1, w2, p0, p1, p2, o_ref,
-    heads, pieces, own, g_buf, rows_buf, t_buf, b0, b1, b2, c0, c1, c2,
-    rz, ry, uz, uy, vz, vy, local, h_send, h_recv, p_send, p_recv, *sems
+    nz, ny, ne, q_ref, k_ref, v_ref, mask_ref, res_ref, proj_ref, place_ref, gain_ref, w0, w1, w2,
+    o_ref, q_buf, kv_buf, s_buf, a_buf, heads, pieces, own, g_buf, rows_buf, t_buf, b0, b1, b2, c0, c1, c2,
+    rz, ry, uz, uy, vz, vy, local, t_send, t_recv, h_send, h_recv, p_send, p_recv, *sems
 ):
     at = z, y, c = place(ny)
     e = lax.axis_index("exp")
@@ -266,7 +270,7 @@
     loads = [
         pltpu.make_async_copy(src, dst, local.at[2 + i])
         for i, (src, dst) in enumerate(
-            [(w0, b0), (w1, b1), (w2, b2), (p0, c0), (p1, c1), (p2, c2)]
+            [(w0, b0), (w1, b1), (w2, b2)]
         )
     ]
     for copy in loads:
@@ -280,7 +284,16 @@
             if de or dc
         ]
     )
-    sent = swap_heads(ny, ne, a_ref, heads, local.at[0], h_send, h_recv)
+    sent, swaps = swap_tokens(
+        nz, ny, (q_ref, k_ref, v_ref), q_buf, kv_buf, [(w0, c0), (w1, c1), (w2, c2)],
+        t_send, t_recv, local.at[pl.ds(5, 3)],
+    )
+    cut = kv_buf.shape[3] * 3 // 4
+    large = (slice(None), pl.ds(0, cut))
+    small = (slice(None), pl.ds(cut, kv_buf.shape[3] - cut))
+    sent += spread(nz, ny, at, peer, kv_buf, large, small, sems[:10])
+    attend(nz, q_buf, kv_buf, mask_ref, s_buf, a_buf)
+    sent += swap_heads(ny, ne, a_buf, heads, local.at[0], h_send, h_recv)
     hidden = res_ref[...].astype(jnp.float32)
     for i in range(ne):
         for j in range(2):
@@ -305,10 +318,10 @@
     cut = width * 3 // 4
     large = (slice(None), pl.ds(0, cut))
     small = (slice(None), pl.ds(cut, width - cut))
-    sent += spread(nz, ny, at, peer, g_buf, large, small, sems[:10])
+    sent += spread(nz, ny, at, peer, g_buf, large, small, sems[10:20])
     count = rows_buf.shape[0]
     rows_buf[...] = g_buf[...].astype(jnp.float32).reshape(count, width).astype(jnp.bfloat16)
-    for copy in loads:
+    for copy in loads + swaps:
         copy.wait()
     rows = rows_buf[...]
     acts = []
@@ -323,12 +336,14 @@
         terms = terms + jnp.dot(acts[1], c2[:, cols], preferred_element_type=jnp.float32)
         t_buf[:, :, :, cols] = terms.reshape(t_buf.shape[:3] + (step,)).astype(jnp.bfloat16)
     own_rows = jnp.concatenate([own[i].astype(jnp.float32) for i in range(ne)], axis=1)
-    sent += sum_rows(nz, ny, t_buf, own_rows, o_ref, rz, ry, uz, uy, vz, vy, sems[10:])
+    sent += sum_rows(nz, ny, t_buf, own_rows, o_ref, rz, ry, uz, uy, vz, vy, sems[20:])
     for copy in sent:
         copy.wait_send()
 
 
-def rest(attended, residual, out_proj, placing, gain, mine, partner, nz, ny, ne):
+def layer(
+    queries, keys, values, mask, residual, out_proj, placing, gain, mine, nz, ny, ne
+):
     tokens, part = residual.shape
     rows, width = tokens // ne, ne * part
     half = width // 2
@@ -341,9 +356,13 @@
     return pl.pallas_call(
         functools.partial(layer_kernel, nz, ny, ne),
         out_shape=jax.ShapeDtypeStruct((rows, width), jnp.bfloat16),
-        in_specs=[VM] * 5 + [ANY] * 6,
+        in_specs=[VM] * 8 + [ANY] * 3,
         out_specs=VM,
         scratch_shapes=[
+            buf(2, tokens, HD),
+            buf(nz, ny, 2, tokens, 2 * HD),
+            pltpu.VMEM((2 * tokens, mask.shape[1]), jnp.float32),
+            buf(2, tokens, HD),
             buf(ne, 2, tokens, HD),
             buf(ne, rows, part),
             buf(ne, rows, part),
@@ -359,59 +378,31 @@
             buf(ny, rows, half),
             buf(nz, rows, half),
             DMA((8,)),
+            DMA((6,)),
+            DMA((6,)),
             DMA((ne, 2)),
             DMA((ne, 2)),
             DMA((ne,)),
             DMA((ne,)),
             *ring_sems(nz, ny),
+            *ring_sems(nz, ny),
             *(DMA((n,)) for n in (nz, nz, ny, ny, ny, ny, nz, nz)),
         ],
-        compiler_params=pltpu.CompilerParams(collective_id=1, has_side_effects=True),
-    )(attended, residual, out_proj, placing, gain, *mine, *partner)
+        compiler_params=pltpu.CompilerParams(collective_id=0, has_side_effects=True),
+    )(queries, keys, values, mask, residual, out_proj, placing, gain, *mine)
 
 
 def body(
     residual, queries, keys, values, out_proj, norm_gain, w_gate, w_up, w_down, routes, block_mask
 ):
     local_tokens = residual.shape[0]
-    blocks_all = block_mask.shape[0]
     expert_count = lax.axis_size("exp")
     ny = ROWS_Y
     nz = lax.axis_size("ctx") // (2 * ny)
     per_expert = local_tokens // expert_count
-    scaling = 1.0 / math.sqrt(HD)
-    ctx_place = lax.axis_index("ctx")
-    q2 = queries.reshape(local_tokens, 2, HD).transpose(1, 0, 2)
-    kv2 = jnp.concatenate(
-        [
-            keys.reshape(local_tokens, 2, HD).transpose(1, 0, 2),
-            values.reshape(local_tokens, 2, HD).transpose(1, 0, 2),
-        ],
-        axis=2,
-    )
-    mine = (w_gate[0], w_up[0], w_down[0])
-    q_chip, kv_all, *partner = gather_keys(q2, kv2, mine, nz, ny)
-    chip_tokens = 2 * local_tokens
-    q_chip = q_chip.reshape(chip_tokens, HD)
-    kv_all = kv_all.reshape(-1, 2 * HD)
-    count = kv_all.shape[0]
-    query_pos = (ctx_place // 2) * chip_tokens + jnp.arange(chip_tokens, dtype=jnp.int32)
-    query_blocks = jax.nn.one_hot(query_pos // BLK, blocks_all, dtype=jnp.float32)
-    query_mask = jnp.dot(query_blocks, block_mask.astype(jnp.float32))
-    key_pos = jnp.arange(count, dtype=jnp.int32)
-    key_blocks = jax.nn.one_hot(key_pos // BLK, blocks_all, dtype=jnp.float32)
-    allowed = jnp.dot(query_mask, key_blocks.T) > 0.5
-    scores = (
-        jnp.einsum("qd,kd->qk", q_chip, kv_all[:, :HD], preferred_element_type=jnp.float32) * scaling
-    )
-    scores = jnp.where(allowed, scores, -1e30)
-    top = jnp.max(scores, axis=1, keepdims=True)
-    exponent = jnp.where(allowed, jnp.exp(scores - top), 0.0)
-    total = jnp.sum(exponent, axis=1, keepdims=True)
-    product = jnp.dot(
-        exponent.astype(jnp.bfloat16), kv_all[:, HD:], preferred_element_type=jnp.float32
-    )
-    attended = (product / total).astype(jnp.bfloat16).reshape(2, local_tokens, HD)
+    chip = lax.axis_index("ctx") // 2
+    assert 2 * local_tokens == BLK
+    mask = jnp.repeat(lax.dynamic_slice_in_dim(block_mask, chip, 1, 0), BLK, axis=1)
     target = routes[:, 0]
     token_ids = jnp.arange(local_tokens, dtype=jnp.int32)
     earlier = (target[:, None] == target[None, :]) & (token_ids[None, :] < token_ids[:, None])
@@ -419,8 +410,10 @@
     slot_of = target * per_expert + ranking
     slot_ids = jnp.arange(expert_count * per_expert, dtype=jnp.int32)
     placing = (slot_of[None, :] == slot_ids[:, None]).astype(jnp.bfloat16)
-    return rest(
-        attended, residual, out_proj, placing, norm_gain[None], mine, partner, nz, ny, expert_count
+    mine = (w_gate[0], w_up[0], w_down[0])
+    return layer(
+        queries, keys, values, mask, residual, out_proj, placing, norm_gain[None], mine, nz, ny,
+        expert_count,
     )[None]
 
 

time: 111 us -> 100 us (0.901)
  the two profiles are of different devices: /device:TPU:8 before, /device:TPU:16 now
where the time goes in v5:
time: 100 us; the launch traced here: 99.8 us
  Pallas kernels  95.5 us (96%)
  local copies, waits for them, and re-layouts  3.43 us (3%)
    pallas_call x1, Pallas kernels, layer(): pl.pallas_call(functools.partial(layer_kernel, nz, ny, ne), out_shape=jax...  95.5 us
    unnamed x5, local copies, waits for them, and re-layouts  2.75 us

profile of v5, /device:TPU:16, one launch (start us, length us, event | category | flops | bytes accessed | tf_op | source)
XLA Modules:
  0.0 99.8 jit_solution(17633013167088619719)
XLA Ops:
  0.0 0.0 copy-start
  0.0 0.7 copy-done
  0.7 0.0 copy-start.1
  0.7 0.7 copy-done.1
  1.4 0.2 convert_reduce_fusion
  1.6 0.6 fusion.1.place_ref
  2.2 0.7 broadcast_in_dim.15
  2.9 95.5 %shard_map.109 = bf16[8,2048]{1,0:T(8,128)(2,1)} custom-call(bf16[64,256]{1,0:T(8,128)(2,1)} %q_ref.1, bf16[64,256]{1,0:T(8,128)(2,1)} %k_ref.1, bf16[64,256]{1,0:T(8,128)(2,1)} %v_ref.1, s32[1,4096]{1,0:T(1,128)} %bitcast.14, bf16[64,256]{1,0:T(8,128)(2,1)} %res_ref.1, bf16[2048,256]{1,0:T(8,128)(2,1)} %proj_ref.1, bf16[64,64]{1,0:T(8,128)(2,1)} %fusion.1.place_ref, ...), custom_call_target="tpu_custom_call" | custom-call | tf_op jit(solution)/shard_map/pallas_call | solution.py:356
  98.4 1.4 %copy.13 = bf16[1,8,2048]{2,1,0:T(8,128)(2,1)} copy(bf16[1,8,2048]{2,1,0:T(8,128)(2,1)} %bitcast.13) | data formatting | bytes 65536
  (2 shorter events, 0.0 us)
Async XLA Ops:
  0.0 0.7 copy-start
  0.7 0.7 copy-start.1

commit v6 on v5

--- a/solution.py
+++ b/solution.py
@@ -40,7 +40,6 @@
     y_send, y_recv, f_send, f_recv, b_send, b_recv, sz_send, sz_recv, sy_send, sy_recv = sems
     up, down = peer(lax.rem(z + 1, nz), y, c), peer(lax.rem(z + nz - 1, nz), y, c)
     half = nz // 2
-    pair = ny // 2
     far_z = sorted(range(1, nz), key=lambda d: -min(d, nz - d))
     far_y = sorted(range(1, ny), key=lambda d: -min(d, ny - d))
     pending = []
@@ -57,24 +56,37 @@
         go(g_ref.at[(z, y) + large], y_send.at[d], y_recv.at[d], peer(z, lax.rem(y + d, ny), c))
     for d in far_z:
         go(g_ref.at[(z, y) + small], sz_send.at[d], sz_recv.at[d], peer(lax.rem(z + d, nz), y, c))
-    for d in reversed(far_y):
-        yy = lax.rem(y + ny - d, ny)
-        arrived(g_ref.at[(z, yy) + large], y_send.at[d], y_recv.at[d], peer(z, yy, c))
+    near_y = [0] + far_y[::-1]
+    ahead = near_y[: ny // 2]
 
     def piece(s, k):
-        return g_ref.at[(lax.rem(z + nz + s, nz), pl.ds(k * pair, pair)) + large]
+        return g_ref.at[(lax.rem(z + nz + s, nz), lax.rem(y + ny - k, ny)) + large]
 
     def onward(s, k):
-        if s < half - 1 or (s == half - 1 and k == 0):
+        if s < half - 1 or (s == half - 1 and k in ahead):
             go(piece(-s, k), f_send.at[s, k], f_recv.at[s, k], up)
 
     def backward(s, k):
-        if s < half - 1 or (s == half - 1 and k == 1):
+        if s < half - 1 or (s == half - 1 and k not in ahead):
             go(piece(s, k), b_send.at[s, k], b_recv.at[s, k], down)
 
-    for k in range(2):
-        onward(0, k)
-        backward(0, k)
+    def relay(s, k):
+        if s == 0:
+            if k:
+                who = peer(z, lax.rem(y + ny - k, ny), c)
+                arrived(piece(0, k), y_send.at[k], y_recv.at[k], who)
+            onward(s, k)
+            backward(s, k)
+        else:
+            if s < half or k in ahead:
+                arrived(piece(-s, k), f_send.at[s - 1, k], f_recv.at[s - 1, k], down)
+                onward(s, k)
+            if s < half or k not in ahead:
+                arrived(piece(s, k), b_send.at[s - 1, k], b_recv.at[s - 1, k], up)
+                backward(s, k)
+
+    for k in near_y:
+        relay(0, k)
     for d in reversed(far_z):
         zz = lax.rem(z + nz - d, nz)
         arrived(g_ref.at[(zz, y) + small], sz_send.at[d], sz_recv.at[d], peer(zz, y, c))
@@ -82,13 +94,8 @@
         ref = g_ref.at[(slice(None), y) + small]
         go(ref, sy_send.at[d], sy_recv.at[d], peer(z, lax.rem(y + d, ny), c))
     for s in range(1, half + 1):
-        for k in range(2):
-            if s < half or k == 0:
-                arrived(piece(-s, k), f_send.at[s - 1, k], f_recv.at[s - 1, k], down)
-                onward(s, k)
-            if s < half or k == 1:
-                arrived(piece(s, k), b_send.at[s - 1, k], b_recv.at[s - 1, k], up)
-                backward(s, k)
+        for k in near_y:
+            relay(s, k)
     for d in reversed(far_y):
         yy = lax.rem(y + ny - d, ny)
         ref = g_ref.at[(slice(None), yy) + small]
@@ -165,7 +172,7 @@
 
 
 def ring_sems(nz, ny):
-    return [DMA((ny,))] * 2 + [DMA((nz // 2, 2))] * 4 + [DMA((nz,))] * 2 + [DMA((ny,))] * 2
+    return [DMA((ny,))] * 2 + [DMA((nz // 2, ny))] * 4 + [DMA((nz,))] * 2 + [DMA((ny,))] * 2
 
 
 def swap_heads(ny, ne, a_ref, o_ref, own, send, recv):

time: 100 us -> 96.6 us (0.966)
  the two profiles are of different devices: /device:TPU:16 before, /device:TPU:4 now
where the time goes in v6:
time: 96.6 us; the launch traced here: 96.3 us
  Pallas kernels  92.1 us (95%)
  local copies, waits for them, and re-layouts  3.43 us (4%)
    pallas_call x1, Pallas kernels, layer(): pl.pallas_call(functools.partial(layer_kernel, nz, ny, ne), out_shape=jax...  92.1 us
    unnamed x5, local copies, waits for them, and re-layouts  2.75 us

profile of v6, /device:TPU:4, one launch (start us, length us, event | category | flops | bytes accessed | tf_op | source)
XLA Modules:
  0.0 96.3 jit_solution(5903888607518159257)
XLA Ops:
  0.0 0.0 copy-start
  0.0 0.7 copy-done
  0.7 0.0 copy-start.1
  0.7 0.7 copy-done.1
  1.4 0.2 convert_reduce_fusion
  1.6 0.6 fusion.1.place_ref
  2.2 0.7 broadcast_in_dim.15
  2.9 92.1 %shard_map.109 = bf16[8,2048]{1,0:T(8,128)(2,1)} custom-call(bf16[64,256]{1,0:T(8,128)(2,1)} %q_ref.1, bf16[64,256]{1,0:T(8,128)(2,1)} %k_ref.1, bf16[64,256]{1,0:T(8,128)(2,1)} %v_ref.1, s32[1,4096]{1,0:T(1,128)} %bitcast.14, bf16[64,256]{1,0:T(8,128)(2,1)} %res_ref.1, bf16[2048,256]{1,0:T(8,128)(2,1)} %proj_ref.1, bf16[64,64]{1,0:T(8,128)(2,1)} %fusion.1.place_ref, ...), custom_call_target="tpu_custom_call" | custom-call | tf_op jit(solution)/shard_map/pallas_call | solution.py:363
  94.9 1.4 %copy.13 = bf16[1,8,2048]{2,1,0:T(8,128)(2,1)} copy(bf16[1,8,2048]{2,1,0:T(8,128)(2,1)} %bitcast.13) | data formatting | bytes 65536
  (2 shorter events, 0.0 us)
Async XLA Ops:
  0.0 0.7 copy-start
  0.7 0.7 copy-start.1
